TPU v7x, 32 devices: a whole 2x2x4 slice. The times are simulated.
32 devices in a mesh: req: 8 (over z, x), tp: 4 (over y, core).
Axes of the slice: x: 2, y: 2, z: 4, core: 2. Of those that a mesh axis runs over, the one named last changes fastest.
Arguments:
- hidden_in: bfloat16 [1024, 4096], P(('req', 'tp')), may hold values from -6 to 6
- queries: bfloat16 [1024, 4096], P(('req', 'tp')), may hold values from -6 to 6
- new_keys: bfloat16 [1024, 1024], P(('req', 'tp')), may hold values from -6 to 6
- new_values: bfloat16 [1024, 1024], P(('req', 'tp')), may hold values from -6 to 6
- key_cache: bfloat16 [32768, 1024], P(('req', 'tp'))
- value_cache: bfloat16 [32768, 1024], P(('req', 'tp')), may hold values from -6 to 6
- cache_lengths: int32 [16], replicated, may hold values from 256 to 2048, as said below
- parent_ids: int32 [16, 64], replicated, may hold values from 0 to 62, as said below
- accepted_leaf: int32 [16], replicated, may hold values from 0 to 63
- query_gain: bfloat16 [128], replicated, may hold values from 0.5 to 1.5
- key_gain: bfloat16 [128], replicated, may hold values from 0.5 to 1.5
- post_gain: bfloat16 [4096], replicated, may hold values from 0.5 to 1.5
- out_weight: bfloat16 [4096, 4096], P('req', 'tp'), may hold values from -0.09375 to 0.09375
- gate_weight: bfloat16 [4096, 6144], P('req', 'tp'), may hold values from -0.09375 to 0.09375
- up_weight: bfloat16 [4096, 6144], P('req', 'tp'), may hold values from -0.09375 to 0.09375
- down_weight: bfloat16 [6144, 4096], P('tp', 'req'), may hold values from -0.078125 to 0.078125
Outputs:
- layer_out: bfloat16 [1024, 4096], P(('req', 'tp'))
- accepted_kv: bfloat16 [1024, 2048], P(('req', 'tp'))
Inputs may be any that keep to these rules, and one draw needn't show every extreme that they name: `cache_lengths`: some request has exactly 2048 live positions and some exactly 256. parent_ids[r, 0] = 0; every other node j has a parent among nodes j - 4 to j - 1.
All inputs are finite; a program needn't handle non-finite values.
Results may differ from a plain program's by a relative error of at most 0.018.
Values may be sent and summed in bfloat16 or wider, within the bound.
A program may use at most 128 MiB of HBM per device.

v0:
```python
import jax
import jax.numpy as jnp
from jax import lax
from jax.sharding import PartitionSpec as P

HEADS = 32
KV_HEADS = 8
HEAD_DIM = 128


NEG = -1e30
EPS = 1e-06
ROPE_BASE = 1000000.0


def swapped(value, axis, bit):
    mask = 2**bit
    pairs = [(source, source ^ mask) for source in range(lax.axis_size(axis))]
    return lax.ppermute(value, axis, pairs)


def head_norm(values, gain_vec):
    mean_sq = jnp.mean(values * values, axis=-1, keepdims=True)
    return values * lax.rsqrt(mean_sq + EPS) * gain_vec.astype(jnp.float32)


def rotate(values, position):
    head_width = values.shape[-1]
    half_width = head_width // 2
    frequency = ROPE_BASE ** (-2.0 * jnp.arange(half_width, dtype=jnp.float32) / head_width)
    angles = position[:, None] * frequency[None, :]
    cosine = jnp.cos(angles)[:, None, :]
    sine_part = jnp.sin(angles)[:, None, :]
    front_half = values[..., :half_width]
    back_half = values[..., half_width:]
    return jnp.concatenate(
        [front_half * cosine - back_half * sine_part, back_half * cosine + front_half * sine_part],
        axis=-1,
    )


def ancestors(parent_row):
    node_count = parent_row.shape[0]
    node_ids = jnp.arange(node_count, dtype=jnp.int32)
    identity_mat = (node_ids[:, None] == node_ids[None, :]).astype(jnp.float32)
    parent_mat = (parent_row[:, None] == node_ids[None, :]).astype(jnp.float32) * (
        1.0 - identity_mat
    )
    reached = jnp.minimum(identity_mat + parent_mat, 1.0)
    for sweep in range(node_count.bit_length()):
        reached = jnp.minimum(jnp.dot(reached, reached, precision=lax.Precision.HIGHEST), 1.0)
    return reached


def per_device(
    hidden_in,
    queries,
    new_keys,
    new_values,
    key_cache,
    value_cache,
    cache_lengths,
    parent_ids,
    accepted_leaf,
    query_gain,
    key_gain,
    post_gain,
    out_weight,
    gate_weight,
    up_weight,
    down_weight,
):
    half_rows = queries.shape[0]
    tree_size = 2 * half_rows
    group_size = HEADS // KV_HEADS
    kv_width = new_keys.shape[1]
    q_width = queries.shape[1]
    score_scale = HEAD_DIM ** (-0.5)
    tp_count = lax.axis_size("tp")
    device = lax.axis_index(("req", "tp"))
    request = device // 2
    pair_side = lax.axis_index("tp") % 2
    cache_length = lax.dynamic_index_in_dim(cache_lengths, request, 0, keepdims=False)
    parent_row = lax.dynamic_index_in_dim(parent_ids, request, 0, keepdims=False)
    leaf_index = lax.dynamic_index_in_dim(accepted_leaf, request, 0, keepdims=False)
    reached = ancestors(parent_row)
    node_depth = jnp.sum(reached, axis=1) - 1.0
    node_ids = jnp.arange(tree_size, dtype=jnp.int32)
    local_ids = jnp.arange(half_rows, dtype=jnp.int32)
    node_order = jnp.concatenate(
        [pair_side * half_rows + local_ids, (1 - pair_side) * half_rows + local_ids]
    )
    reorder = (node_order[:, None] == node_ids[None, :]).astype(jnp.float32)
    reached_rows = jnp.dot(reorder, reached, precision=lax.Precision.HIGHEST)
    own_cols = jnp.dot(reached_rows, reorder[:half_rows].T, precision=lax.Precision.HIGHEST) > 0.5
    own_depth = jnp.dot(reorder[:half_rows], node_depth, precision=lax.Precision.HIGHEST)
    position = cache_length.astype(jnp.float32) + own_depth
    query_heads = rotate(
        head_norm(queries.astype(jnp.float32).reshape(half_rows, HEADS, HEAD_DIM), query_gain),
        position,
    ).astype(jnp.bfloat16)
    key_heads = rotate(
        head_norm(new_keys.astype(jnp.float32).reshape(half_rows, KV_HEADS, HEAD_DIM), key_gain),
        position,
    ).astype(jnp.bfloat16)
    query_own = query_heads.reshape(half_rows, q_width)
    fresh_own = jnp.concatenate([key_heads.reshape(half_rows, kv_width), new_values], axis=1)
    query_other, fresh_other = swapped((query_own, fresh_own), "tp", 0)
    query_all = jnp.concatenate([query_own, query_other], axis=0).reshape(
        tree_size, KV_HEADS, group_size, HEAD_DIM
    )

    def attend(running, block_keys, block_values, allowed):
        run_top, run_total, summed = running
        scores = (
            jnp.einsum("qhgd,khd->hgqk", query_all, block_keys, preferred_element_type=jnp.float32)
            * score_scale
        )
        scores = jnp.where(allowed, scores, NEG)
        new_top = jnp.maximum(run_top, jnp.max(scores, axis=-1, keepdims=True))
        weights = jnp.where(allowed, jnp.exp(scores - new_top), 0.0).astype(jnp.bfloat16)
        shrink = jnp.exp(run_top - new_top)
        run_total = run_total * shrink + jnp.sum(
            weights.astype(jnp.float32), axis=-1, keepdims=True
        )
        summed = summed * shrink + jnp.einsum(
            "hgqk,khd->hgqd", weights, block_values, preferred_element_type=jnp.float32
        )
        return (new_top, run_total, summed)

    shard_rows = key_cache.shape[0]
    block_rows = shard_rows // 8
    key_blocks = key_cache.reshape(8, block_rows, KV_HEADS, HEAD_DIM)
    value_blocks = value_cache.reshape(8, block_rows, KV_HEADS, HEAD_DIM)
    first_block = pair_side * 8
    stride = 1
    needed = (cache_length + block_rows - 1) // block_rows
    live_blocks = jnp.clip((needed - first_block + stride - 1) // stride, 0, 8)

    def cache_step(block_index, running):
        block_keys = lax.dynamic_index_in_dim(key_blocks, block_index, 0, keepdims=False)
        block_values = lax.dynamic_index_in_dim(value_blocks, block_index, 0, keepdims=False)
        first_slot = (first_block + stride * block_index) * block_rows
        allowed = first_slot + jnp.arange(block_rows, dtype=jnp.int32) < cache_length
        allowed = jnp.broadcast_to(allowed[None, :], (tree_size, block_rows))
        return attend(running, block_keys, block_values, allowed)

    initial = (
        jnp.full((KV_HEADS, group_size, tree_size, 1), NEG, jnp.float32),
        jnp.zeros((KV_HEADS, group_size, tree_size, 1), jnp.float32),
        jnp.zeros((KV_HEADS, group_size, tree_size, HEAD_DIM), jnp.float32),
    )
    running = lax.fori_loop(0, live_blocks, cache_step, initial)
    running = attend(
        running, key_heads, new_values.reshape(half_rows, KV_HEADS, HEAD_DIM), own_cols
    )
    run_top, run_total, summed = running
    far_top, far_total, far_sum = (
        swapped(run_top[:, :, half_rows:].astype(jnp.bfloat16), "tp", 0).astype(jnp.float32),
        swapped(run_total[:, :, half_rows:].astype(jnp.bfloat16), "tp", 0).astype(jnp.float32),
        swapped(summed[:, :, half_rows:].astype(jnp.bfloat16), "tp", 0).astype(jnp.float32),
    )
    near_top = run_top[:, :, :half_rows]
    joint_top = jnp.maximum(near_top, far_top)
    near_scale = jnp.exp(near_top - joint_top)
    far_scale = jnp.exp(far_top - joint_top)
    denominator = run_total[:, :, :half_rows] * near_scale + far_total * far_scale
    merged = (summed[:, :, :half_rows] * near_scale + far_sum * far_scale) / denominator
    attended = jnp.transpose(merged, (2, 0, 1, 3)).reshape(half_rows, q_width).astype(jnp.bfloat16)
    leaf_pick = (node_ids == leaf_index).astype(jnp.float32)
    leaf_row = jnp.dot(leaf_pick, reached, precision=lax.Precision.HIGHEST)
    out_depths = (pair_side * half_rows + local_ids).astype(jnp.float32)
    chosen = leaf_row[None, :] * (node_depth[None, :] == out_depths[:, None]).astype(jnp.float32)
    chosen = jnp.dot(chosen, reorder.T, precision=lax.Precision.HIGHEST)
    fresh_all = jnp.concatenate([fresh_own, fresh_other], axis=0)
    accepted_kv = jnp.dot(
        chosen.astype(jnp.bfloat16), fresh_all, preferred_element_type=jnp.float32
    ).astype(jnp.bfloat16)
    attn_group = lax.all_gather(attended, "tp", axis=0, tiled=True)
    group_rows = attn_group.shape[0]
    projected = jnp.dot(
        attn_group,
        lax.all_gather(out_weight, "req", axis=0, tiled=True),
        preferred_element_type=jnp.float32,
    )
    own_projected = lax.all_to_all(
        projected.astype(jnp.bfloat16), "tp", split_axis=0, concat_axis=1, tiled=True
    ).astype(projected.dtype)
    residual = (hidden_in.astype(jnp.float32) + own_projected).astype(jnp.bfloat16)
    residual_wide = residual.astype(jnp.float32)
    mean_sq = jnp.mean(residual_wide * residual_wide, axis=-1, keepdims=True)
    normed = (residual_wide * lax.rsqrt(mean_sq + EPS) * post_gain.astype(jnp.float32)).astype(
        jnp.bfloat16
    )
    normed_group = lax.all_gather(normed, "tp", axis=0, tiled=True)
    split_width = gate_weight.shape[1] // 2
    req_count = lax.axis_size("req")

    def doubled_rows(shard):
        stacked_halves = jnp.concatenate([shard[:, :split_width], shard[:, split_width:]], axis=0)
        return jnp.tile(stacked_halves, (req_count // 2, 1))

    gate_full, up_full = (
        lax.all_to_all(doubled_rows(gate_weight), "req", split_axis=0, concat_axis=0, tiled=True),
        lax.all_to_all(doubled_rows(up_weight), "req", split_axis=0, concat_axis=0, tiled=True),
    )
    down_halves = jnp.concatenate([down_weight[:split_width], down_weight[split_width:]], axis=1)
    down_full = lax.all_to_all(
        jnp.tile(down_halves, (1, req_count // 2)), "req", split_axis=1, concat_axis=1, tiled=True
    )
    partner_rows = swapped(normed_group, "req", 0)
    stacked_rows = jnp.stack([normed_group, partner_rows]).reshape(
        2, tp_count, half_rows, normed_group.shape[1]
    )
    rows_all = jnp.transpose(stacked_rows, (1, 0, 2, 3)).reshape(
        2 * group_rows, normed_group.shape[1]
    )
    gate_sum = jnp.dot(rows_all, gate_full, preferred_element_type=jnp.float32)
    up_sum = jnp.dot(rows_all, up_full, preferred_element_type=jnp.float32)
    hidden = (jax.nn.silu(gate_sum) * up_sum).astype(jnp.bfloat16)
    partial_out = jnp.dot(hidden, down_full, preferred_element_type=jnp.float32)
    paired_sum = lax.psum_scatter(
        partial_out.astype(jnp.bfloat16), "tp", scatter_dimension=0, tiled=True
    ).astype(jnp.float32)
    returned = swapped(paired_sum[half_rows:].astype(jnp.bfloat16), "req", 0).astype(jnp.float32)
    mlp_own = paired_sum[:half_rows] + returned
    layer_out = (residual_wide + mlp_own).astype(jnp.bfloat16)
    return (layer_out, accepted_kv)


def solution(mesh):
    in_specs = (
        P(("req", "tp"), None),
        P(("req", "tp"), None),
        P(("req", "tp"), None),
        P(("req", "tp"), None),
        P(("req", "tp"), None),
        P(("req", "tp"), None),
        P(),
        P(),
        P(),
        P(),
        P(),
        P(),
        P("req", "tp"),
        P("req", "tp"),
        P("req", "tp"),
        P("tp", "req"),
    )
    out_specs = (P(("req", "tp"), None), P(("req", "tp"), None))
    return jax.shard_map(
        per_device, mesh=mesh, in_specs=in_specs, out_specs=out_specs, check_vma=False
    )
```

profile of v0, /device:TPU:0, one launch (start us, length us, event | category | flops | bytes accessed | tf_op | source)
XLA Modules:
  0.0 613.6 jit_solution(6316733818064254265)
XLA Ops:
  9.2 1.3 dynamic_slice.18
  15.1 3.0 tile.6
  18.1 6.9 %all-to-all-start.1 = ((bf16[8,512,768]{2,1,0:T(8,128)(2,1)}), bf16[8,512,768]{2,1,0:T(8,128)(2,1)}, u32[]{:S(2)}, u32[]{:S(2)}) async-start(bf16[8,512,768]{2,1,0:T(8,128)(2,1)} %bitcast.156), calls=%async_computation.1 | async-start | bytes 12582912 | tf_op jit(solution)/shard_map/all_to_all | solution.py:204
  26.6 2.0 copy.89
  28.6 2.0 copy.92
  31.9 11.4 %while.14 = (s32[]{:T(128)}, f32[8,4,64,1]{2,1,0,3:T(4,128)S(1)}, f32[8,4,64,1]{2,1,0,3:T(4,128)S(1)}, f32[8,4,64,128]{3,2,1,0:T(8,128)S(1)}, s32[]{:T(128)}, /*...) while((s32[]{:T(128)}, f32[8,4,64,1]{2,1,0,3:T(4,128)S(1)}, ...), condition=%wide.region_5.6_spmd, body=%wide.region_2.5_spmd.sunk | while | flops 137632000 | bytes 7471819 | solution.py:153
  31.9 1.1 constant_dynamic-slice_fusion.3
  35.7 1.1 constant_dynamic-slice_fusion.3
  49.3 3.0 tile.8
  52.3 8.7 %copy.74 = bf16[768,8,512]{2,0,1:T(8,128)(2,1)} copy(bf16[768,8,512]{0,2,1:T(8,128)(2,1)} %bitcast.158) | data formatting | bytes 12582912 | tf_op jit(solution)/shard_map/all_to_all | solution.py:208
  61.1 166.0 %all-to-all-done.1 = bf16[8,512,768]{2,1,0:T(8,128)(2,1)} async-done(((bf16[8,512,768]{2,1,0:T(8,128)(2,1)}), bf16[8,512,768]{2,1,0:T(8,128)(2,1)}, u32[]{:S(2)}, u32[]{:S(2)}) %all-to-all-start.1) | async-done | bytes 6291488 | tf_op jit(solution)/shard_map/all_to_all | solution.py:204
  227.1 4.7 all-to-all-start.3
  231.8 70.0 %all-gather.6.cloned.1.call-done = bf16[4096,1024]{1,0:T(8,128)(2,1)} async-done(((bf16[512,1024]{1,0:T(8,128)(2,1)}), bf16[4096,1024]{1,0:T(8,128)(2,1)}) %all-gather.6.cloned.1.call-update) | async-done | bytes 8388624 | tf_op jit(solution)/shard_map/all_gather | solution.py:183
  301.8 5.7 convolution_convert_fusion.2
  307.5 92.8 %all-to-all-done.3 = bf16[768,8,512]{2,0,1:T(8,128)(2,1)} async-done(((bf16[768,8,512]{2,0,1:T(8,128)(2,1)}), bf16[768,8,512]{2,0,1:T(8,128)(2,1)}, u32[]{:S(2)}, u32[]{:S(2)}) %all-to-all-start.3) | async-done | bytes 6291488 | tf_op jit(solution)/shard_map/all_to_all | solution.py:208
  400.2 3.6 all-to-all-start
  404.1 5.6 all-to-all-done
  409.7 3.1 tile.7
  412.8 4.9 all-to-all-start.2
  419.0 18.8 %all-gather.8.cloned.1.call-done = bf16[128,4096]{1,0:T(8,128)(2,1)} async-done(((bf16[32,4096]{1,0:T(8,128)(2,1)}), bf16[128,4096]{1,0:T(8,128)(2,1)}) %all-gather.8.cloned.1.call-update) | async-done | bytes 1048592 | tf_op jit(solution)/shard_map/all_gather | solution.py:195
  437.8 1.5 collective-permute-start.4
  439.2 8.6 %copy.75 = bf16[768,8,512]{0,2,1:T(8,128)(2,1)} copy(bf16[768,8,512]{2,0,1:T(8,128)(2,1)} %all-to-all-done.3) | data formatting | bytes 12582912 | tf_op jit(solution)/shard_map/all_to_all | solution.py:208
  447.9 62.8 %collective-permute-done.4 = bf16[128,4096]{1,0:T(8,128)(2,1)S(1)} collective-permute-done((bf16[128,4096]{1,0:T(8,128)(2,1)}, bf16[128,4096]{1,0:T(8,128)(2,1)S(1)}, u32[]{:S(2)}, u32[]{:S(2)}) %collective-permute-start.4) | collective-permute-done | bytes 1048608 | tf_op jit(solution)/shard_map/ppermute | solution.py:19
  510.6 1.1 copy-done.8
  511.7 1.4 pad_maximum_fusion
  513.2 4.6 fusion.67
  517.8 38.1 %all-to-all-done.2 = bf16[8,512,768]{2,1,0:T(8,128)(2,1)} async-done(((bf16[8,512,768]{2,1,0:T(8,128)(2,1)}), bf16[8,512,768]{2,1,0:T(8,128)(2,1)}, u32[]{:S(2)}, u32[]{:S(2)}) %all-to-all-start.2) | async-done | bytes 6291488 | tf_op jit(solution)/shard_map/all_to_all | solution.py:205
  555.8 10.7 %convolution_convert_fusion = bf16[256,4096]{1,0:T(8,128)(2,1)} fusion(bf16[768,4096]{0,1:T(8,128)(2,1)} %bitcast.161, f32[256,768]{1,0:T(8,128)S(1)} %fusion.67, bf16[256,4096]{1,0:T(8,128)(2,1)S(1)} %bitcast.169, bf16[4096,768]{1,0:T(8,128)(2,1)} %bitcast.40), kind=kOutput, calls=%fused_computation.16 | convolution fusion | flops 3223453696 | bytes 17563648 | tf_op jit(solution)/shard_map/dot_general | solution.py:221
  568.9 27.3 %reduce-scatter.2.cloned.1.call-done = bf16[64,4096]{1,0:T(8,128)(2,1)} async-done(((bf16[256,4096]{1,0:T(8,128)(2,1)}), bf16[64,4096]{1,0:T(8,128)(2,1)}) %reduce-scatter.2.cloned.1.call-update) | async-done | bytes 524304 | tf_op jit(solution)/shard_map/reduce_scatter | solution.py:222
  597.2 1.5 collective-permute-start.5
  599.8 5.5 collective-permute-done.5
  605.3 1.8 fusion.10
  (155 shorter events, 28.7 us)
Async XLA Ops:
  7.2 5.5 copy-start.17
  12.6 2.2 copy-start.4
  14.4 16.3 %collective-permute-start = (bf16[32,4096]{1,0:T(8,128)(2,1)}, bf16[32,4096]{1,0:T(8,128)(2,1)S(1)}, u32[]{:S(2)}, u32[]{:S(2)}) collective-permute-start(bf16[32,4096]{1,0:T(8,128)(2,1)} %bitcast.143), channel_id=1, source_target_pairs={{0,1},{1,0},{2,3},{3,2},{4,5},{5,4},{6,7},{7,6},{8,9},{9,8},{10,11... | collective-permute-start | bytes 786440 | tf_op jit(solution)/shard_map/ppermute | solution.py:19
  18.1 7.0 %copy-start.15 = (bf16[32,1024]{1,0:T(8,128)(2,1)S(1)}, bf16[32,1024]{1,0:T(8,128)(2,1)}, u32[]{:S(2)}) copy-start(bf16[32,1024]{1,0:T(8,128)(2,1)} %param.20) | copy-start | bytes 196612
  18.1 7.2 %copy-start.18 = (bf16[128]{0:T(256)(128)(2,1)S(1)}, bf16[128]{0:T(256)(128)(2,1)}, u32[]{:S(2)}) copy-start(bf16[128]{0:T(256)(128)(2,1)} %param.28) | copy-start | bytes 772
  18.1 8.5 %copy-start.2 = (bf16[1024,1024]{1,0:T(8,128)(2,1)S(1)}, bf16[1024,1024]{1,0:T(8,128)(2,1)}, u32[]{:S(2)}) copy-start(bf16[1024,1024]{1,0:T(8,128)(2,1)} %param.22) | copy-start | bytes 6291460
  18.1 209.0 %all-to-all-start.1 = ((bf16[8,512,768]{2,1,0:T(8,128)(2,1)}), bf16[8,512,768]{2,1,0:T(8,128)(2,1)}, u32[]{:S(2)}, u32[]{:S(2)}) async-start(bf16[8,512,768]{2,1,0:T(8,128)(2,1)} %bitcast.156), calls=%async_computation.1 | async-start | bytes 12582912 | tf_op jit(solution)/shard_map/all_to_all | solution.py:204
  25.0 206.8 %all-gather.4.cloned.1.call-start = ((), (), s32[]{:S(2)}) async-start(), calls=%async_computation.5 | async-start | bytes 1310720 | tf_op jit(solution)/shard_map/all_gather | solution.py:179
  26.6 2.0 copy-start.3
  28.6 2.0 copy-start.9
  30.7 1.2 copy-start.10
  30.7 1.2 copy-start.12
  43.8 4.4 copy-start.5
  43.8 2.1 collective-permute-start.2
  44.3 1.3 collective-permute-start.3
  44.8 1.2 collective-permute-start.1
  47.5 254.3 %all-gather.6.cloned.1.call-start = ((), (), s32[]{:S(2)}) async-start(), calls=%async_computation.6 | async-start | bytes 9437184 | tf_op jit(solution)/shard_map/all_gather | solution.py:183
  227.1 173.2 %all-to-all-start.3 = ((bf16[768,8,512]{2,0,1:T(8,128)(2,1)}), bf16[768,8,512]{2,0,1:T(8,128)(2,1)}, u32[]{:S(2)}, u32[]{:S(2)}) async-start(bf16[768,8,512]{2,0,1:T(8,128)(2,1)} %copy.74), calls=%async_computation.3 | async-start | bytes 12582912 | tf_op jit(solution)/shard_map/all_to_all | solution.py:208
  231.8 172.0 %copy-start.6 = (bf16[512,1536]{1,0:T(8,128)(2,1)S(1)}, bf16[512,1536]{1,0:T(8,128)(2,1)}, u32[]{:S(2)}) copy-start(bf16[512,1536]{1,0:T(8,128)(2,1)} %param.32) | copy-start | bytes 4718596
  400.2 9.4 %all-to-all-start = ((bf16[4,32,1024]{2,1,0:T(8,128)(2,1)}), bf16[4,32,1024]{2,1,0:T(8,128)(2,1)S(1)}, u32[]{:S(2)}, u32[]{:S(2)}) async-start(bf16[4,32,1024]{2,1,0:T(8,128)(2,1)} %bitcast.28), calls=%async_computation | async-start | bytes 524288 | tf_op jit(solution)/shard_map/all_to_all | solution.py:186
  412.8 4.9 copy-start.16
  412.8 5.1 copy-start.14
  412.8 143.1 %all-to-all-start.2 = ((bf16[8,512,768]{2,1,0:T(8,128)(2,1)}), bf16[8,512,768]{2,1,0:T(8,128)(2,1)}, u32[]{:S(2)}, u32[]{:S(2)}) async-start(bf16[8,512,768]{2,1,0:T(8,128)(2,1)} %bitcast.157), calls=%async_computation.2 | async-start | bytes 12582912 | tf_op jit(solution)/shard_map/all_to_all | solution.py:205
  417.6 20.1 %all-gather.8.cloned.1.call-start = ((), (), s32[]{:S(2)}) async-start(), calls=%async_computation.7 | async-start | bytes 1310720 | tf_op jit(solution)/shard_map/all_gather | solution.py:195
  418.9 177.4 %reduce-scatter.2.cloned.1.call-start = ((), (), s32[]{:S(2)}) async-start(), calls=%async_computation.8 | async-start | bytes 2621440 | tf_op jit(solution)/shard_map/reduce_scatter | solution.py:222
  437.8 74.0 %copy-start.7 = (bf16[128,4096]{1,0:T(8,128)(2,1)S(1)}, bf16[128,4096]{1,0:T(8,128)(2,1)}, u32[]{:S(2)}) copy-start(bf16[128,4096]{1,0:T(8,128)(2,1)} %all-gather.8.cloned.1.call-done) | copy-start | bytes 3145732
  437.8 72.9 %collective-permute-start.4 = (bf16[128,4096]{1,0:T(8,128)(2,1)}, bf16[128,4096]{1,0:T(8,128)(2,1)S(1)}, u32[]{:S(2)}, u32[]{:S(2)}) collective-permute-start(bf16[128,4096]{1,0:T(8,128)(2,1)} %all-gather.8.cloned.1.call-done), channel_id=1, source_target_pairs={{0,4},{4,0},{8,12},{12,8},{16,20},{20,16},{24,28},{28,24},{1,5},{5... | collective-permute-start | bytes 3145736 | tf_op jit(solution)/shard_map/ppermute | solution.py:19
  510.6 1.1 copy-start.8
  566.5 1.1 copy-start.19
  566.5 40.6 %copy-start.1 = (s32[16,64]{1,0:T(8,128)S(1)}, s32[16,64]{1,0:T(8,128)}, u32[]{:S(2)}) copy-start(s32[16,64]{1,0:T(8,128)} %param.25) | copy-start | bytes 12292
  567.5 31.5 %collective-permute-start.6 = (bf16[32,2048]{1,0:T(8,128)(2,1)S(1)}, bf16[32,2048]{1,0:T(8,128)(2,1)S(1)}, u32[]{:S(2)}, u32[]{:S(2)}) collective-permute-start(bf16[32,2048]{1,0:T(8,128)(2,1)S(1)} %constant_dynamic-update-slice_fusion), channel_id=1, source_target_pairs={{0,1},{1,0},{2,3},{3,2},{4,5},{5,4},{6,7},{7,6},{8,9},{9,8},{10,11... | collective-permute-start | bytes 393224 | tf_op jit(solution)/shard_map/ppermute | solution.py:19
  597.2 8.1 %collective-permute-start.5 = (bf16[32,4096]{1,0:T(8,128)(2,1)S(1)}, bf16[32,4096]{1,0:T(8,128)(2,1)S(1)}, u32[]{:S(2)}, u32[]{:S(2)}) collective-permute-start(bf16[32,4096]{1,0:T(8,128)(2,1)S(1)} %slice.97), channel_id=1, source_target_pairs={{0,4},{4,0},{8,12},{12,8},{16,20},{20,16},{24,28},{28,24},{1,5},{5... | collective-permute-start | bytes 786440 | tf_op jit(solution)/shard_map/ppermute | solution.py:19
  (3 other events, 2.4 us)
Sparse Core Ops, SparseCore 0:
  47.6 37.0 all-gather.3
  86.8 214.9 all-gather.5
  420.6 17.0 all-gather.7
  566.7 29.5 reduce-scatter.1
where the time goes:
time: 615 us; the launch traced here: 614 us
  waiting for transfers between devices  489 us (80%)
  local copies, waits for them, and re-layouts  42.9 us (7%)
  matrix products  29.6 us (5%)
  starting transfers between devices  24.5 us (4%)
  between operations  15.7 us (3%)
  other arithmetic  12.1 us (2%)
    all_to_all x1, waiting for transfers between devices, per_device(): lax.all_to_all(doubled_rows(gate_weight), 'req', split_axis=0, concat_axi...  166 us
    all_to_all x1, waiting for transfers between devices, per_device(): lax.all_to_all(jnp.tile(down_halves, (1, req_count // 2)), 'req', split_a...  92.8 us
    all_gather x1, waiting for transfers between devices, per_device(): lax.all_gather(out_weight, 'req', axis=0, tiled=True)  70 us
    ppermute x7, waiting for transfers between devices, swapped(): return lax.ppermute(value, axis, pairs)  69.4 us
    all_to_all x1, waiting for transfers between devices, per_device(): lax.all_to_all(doubled_rows(up_weight), 'req', split_axis=0, concat_axis=...  38.1 us
    reduce_scatter x1, waiting for transfers between devices, per_device(): lax.psum_scatter(partial_out.astype(jnp.bfloat16), 'tp', scatter_dimensio...  27.3 us
    all_gather x1, waiting for transfers between devices, per_device(): normed_group = lax.all_gather(normed, 'tp', axis=0, tiled=True)  18.8 us
    all_to_all x2, local copies, waits for them, and re-layouts, per_device(): lax.all_to_all(jnp.tile(down_halves, (1, req_count // 2)), 'req', split_a...  17.4 us
  transfers between devices with their start and end apart: 15, of which 11 were waited for; matrix products, arithmetic and copies ran while one was open for 10% of the time, Pallas kernels for 0%

commit v1 on v0

--- a/solution.py
+++ b/solution.py
@@ -176,54 +176,49 @@
     accepted_kv = jnp.dot(
         chosen.astype(jnp.bfloat16), fresh_all, preferred_element_type=jnp.float32
     ).astype(jnp.bfloat16)
-    attn_group = lax.all_gather(attended, "tp", axis=0, tiled=True)
-    group_rows = attn_group.shape[0]
-    projected = jnp.dot(
-        attn_group,
-        lax.all_gather(out_weight, "req", axis=0, tiled=True),
-        preferred_element_type=jnp.float32,
+    req_count = lax.axis_size("req")
+
+    def feature_slices(rows):
+        parts = rows.reshape(half_rows, req_count, -1)
+        parts = jnp.transpose(parts, (1, 0, 2))
+        parts = lax.all_to_all(parts, "req", split_axis=0, concat_axis=0, tiled=True)
+        parts = lax.all_gather(parts[:, None], "tp", axis=1, tiled=True)
+        return parts.reshape(req_count * tp_count * half_rows, -1)
+
+    attn_slice = feature_slices(attended)
+    projected = jnp.dot(attn_slice, out_weight, preferred_element_type=jnp.float32)
+    projected = lax.psum_scatter(
+        projected.astype(jnp.bfloat16), "req", scatter_dimension=0, tiled=True
     )
     own_projected = lax.all_to_all(
-        projected.astype(jnp.bfloat16), "tp", split_axis=0, concat_axis=1, tiled=True
-    ).astype(projected.dtype)
+        projected, "tp", split_axis=0, concat_axis=1, tiled=True
+    ).astype(jnp.float32)
     residual = (hidden_in.astype(jnp.float32) + own_projected).astype(jnp.bfloat16)
     residual_wide = residual.astype(jnp.float32)
     mean_sq = jnp.mean(residual_wide * residual_wide, axis=-1, keepdims=True)
     normed = (residual_wide * lax.rsqrt(mean_sq + EPS) * post_gain.astype(jnp.float32)).astype(
         jnp.bfloat16
     )
-    normed_group = lax.all_gather(normed, "tp", axis=0, tiled=True)
-    split_width = gate_weight.shape[1] // 2
-    req_count = lax.axis_size("req")
-
-    def doubled_rows(shard):
-        stacked_halves = jnp.concatenate([shard[:, :split_width], shard[:, split_width:]], axis=0)
-        return jnp.tile(stacked_halves, (req_count // 2, 1))
-
-    gate_full, up_full = (
-        lax.all_to_all(doubled_rows(gate_weight), "req", split_axis=0, concat_axis=0, tiled=True),
-        lax.all_to_all(doubled_rows(up_weight), "req", split_axis=0, concat_axis=0, tiled=True),
-    )
-    down_halves = jnp.concatenate([down_weight[:split_width], down_weight[split_width:]], axis=1)
-    down_full = lax.all_to_all(
-        jnp.tile(down_halves, (1, req_count // 2)), "req", split_axis=1, concat_axis=1, tiled=True
-    )
-    partner_rows = swapped(normed_group, "req", 0)
-    stacked_rows = jnp.stack([normed_group, partner_rows]).reshape(
-        2, tp_count, half_rows, normed_group.shape[1]
-    )
-    rows_all = jnp.transpose(stacked_rows, (1, 0, 2, 3)).reshape(
-        2 * group_rows, normed_group.shape[1]
-    )
-    gate_sum = jnp.dot(rows_all, gate_full, preferred_element_type=jnp.float32)
-    up_sum = jnp.dot(rows_all, up_full, preferred_element_type=jnp.float32)
+    normed_slice = feature_slices(normed)
+    gate_part = jnp.dot(normed_slice, gate_weight, preferred_element_type=jnp.float32)
+    up_part = jnp.dot(normed_slice, up_weight, preferred_element_type=jnp.float32)
+    gate_sum = lax.psum_scatter(
+        gate_part.astype(jnp.bfloat16), "req", scatter_dimension=0, tiled=True
+    ).astype(jnp.float32)
+    up_sum = lax.psum_scatter(
+        up_part.astype(jnp.bfloat16), "req", scatter_dimension=0, tiled=True
+    ).astype(jnp.float32)
     hidden = (jax.nn.silu(gate_sum) * up_sum).astype(jnp.bfloat16)
-    partial_out = jnp.dot(hidden, down_full, preferred_element_type=jnp.float32)
-    paired_sum = lax.psum_scatter(
-        partial_out.astype(jnp.bfloat16), "tp", scatter_dimension=0, tiled=True
-    ).astype(jnp.float32)
-    returned = swapped(paired_sum[half_rows:].astype(jnp.bfloat16), "req", 0).astype(jnp.float32)
-    mlp_own = paired_sum[:half_rows] + returned
+    hidden_all = lax.all_gather(hidden, "req", axis=0, tiled=True)
+    partial_out = jnp.dot(hidden_all, down_weight, preferred_element_type=jnp.float32)
+    partial_out = partial_out.astype(jnp.bfloat16).reshape(req_count, tp_count, half_rows, -1)
+    partial_out = jnp.transpose(partial_out, (1, 0, 2, 3)).reshape(
+        tp_count * req_count * half_rows, -1
+    )
+    paired_sum = lax.psum_scatter(partial_out, "tp", scatter_dimension=0, tiled=True)
+    mlp_own = lax.all_to_all(
+        paired_sum, "req", split_axis=0, concat_axis=1, tiled=True
+    ).astype(jnp.float32)
     layer_out = (residual_wide + mlp_own).astype(jnp.bfloat16)
     return (layer_out, accepted_kv)
 

time: 615 us -> 480 us (0.78)
  waiting for transfers between devices: 489 us -> 341 us
  blocking collectives: 0 us -> 46.7 us
  local copies, waits for them, and re-layouts: 42.9 us -> 19.2 us
  starting transfers between devices: 24.5 us -> 10.6 us
    all_to_all x4 -> x2, waiting for transfers between devices: 302 us -> 13.8 us  [the longest x1 7.84 us: per_device(): lax.all_to_all(paired_sum, 'req', split_axis=0, concat_axis=1, tiled=True)]
    reduce_scatter x1 -> x4, waiting for transfers between devices: 27.3 us -> 237 us  [the longest x1 77 us: per_device(): lax.psum_scatter(gate_part.astype(jnp.bfloat16), 'req', scatter_dimension...]
    ppermute x7 -> x5, waiting for transfers between devices: 69.4 us -> 1.2 us  [swapped(): return lax.ppermute(value, axis, pairs)]
    all_to_all x0 -> x2, blocking collectives: none -> 46.7 us  [feature_slices(): lax.all_to_all(parts, 'req', split_axis=0, concat_axis=0, tiled=True)]
    all_to_all x2, local copies, waits for them, and re-layouts: 17.4 us -> 1.7 us  [feature_slices(): lax.all_to_all(parts, 'req', split_axis=0, concat_axis=0, tiled=True)]
    all_to_all x4 -> x2, starting transfers between devices: 20.1 us -> 8.91 us  [the longest x1 5.51 us: per_device(): lax.all_to_all(paired_sum, 'req', split_axis=0, concat_axis=1, tiled=True)]
    another operation x3 -> x0, local copies, waits for them, and re-layouts: 9.1 us -> none  [the longest x2 6.1 us: doubled_rows(): return jnp.tile(stacked_halves, (req_count // 2, 1))]
    dot_general x3 -> x4, matrix products: 21 us -> 14.6 us  [the longest x1 4.87 us: per_device(): jnp.dot(normed_slice, gate_weight, preferred_element_type=jnp.float32)]
  transfers between devices with their start and end apart: 15 -> 14, of which waited for: 11 -> 10; matrix products, arithmetic and copies ran while one was open for 10% -> 3% of each run, Pallas kernels for 0% -> 0%
where the time goes in v1:
time: 480 us; the launch traced here: 478 us
  waiting for transfers between devices  341 us (71%)
  blocking collectives  46.7 us (10%)
  matrix products  29.6 us (6%)
  local copies, waits for them, and re-layouts  19.2 us (4%)
  between operations  16.1 us (3%)
  other arithmetic  14.2 us (3%)
  starting transfers between devices  10.6 us (2%)
    reduce_scatter x1, waiting for transfers between devices, per_device(): lax.psum_scatter(gate_part.astype(jnp.bfloat16), 'req', scatter_dimension...  77 us
    reduce_scatter x1, waiting for transfers between devices, per_device(): lax.psum_scatter(up_part.astype(jnp.bfloat16), 'req', scatter_dimension=0...  69.6 us
    reduce_scatter x1, waiting for transfers between devices, per_device(): lax.psum_scatter(projected.astype(jnp.bfloat16), 'req', scatter_dimension...  67.9 us
    all_gather x1, waiting for transfers between devices, per_device(): hidden_all = lax.all_gather(hidden, 'req', axis=0, tiled=True)  59.8 us
    all_to_all x2, blocking collectives, feature_slices(): lax.all_to_all(parts, 'req', split_axis=0, concat_axis=0, tiled=True)  46.7 us
    all_gather x2, waiting for transfers between devices, feature_slices(): parts = lax.all_gather(parts[:, None], 'tp', axis=1, tiled=True)  29.7 us
    reduce_scatter x1, waiting for transfers between devices, per_device(): lax.psum_scatter(partial_out, 'tp', scatter_dimension=0, tiled=True)  22.1 us
  transfers between devices with their start and end apart: 14, of which 10 were waited for; matrix products, arithmetic and copies ran while one was open for 3% of the time, Pallas kernels for 0%

profile of v1, /device:TPU:0, one launch (start us, length us, event | category | flops | bytes accessed | tf_op | source)
XLA Modules:
  0.0 477.9 jit_solution(10783788420115834484)
XLA Ops:
  16.0 3.7 copy.97
  19.7 1.9 copy.100
  23.7 19.2 %while.14 = (s32[]{:T(128)}, f32[8,4,64,1]{2,1,0,3:T(4,128)S(1)}, f32[8,4,64,1]{2,1,0,3:T(4,128)S(1)}, f32[8,4,64,128]{3,2,1,0:T(8,128)S(1)}, s32[]{:T(128)}, /*...) while((s32[]{:T(128)}, f32[8,4,64,1]{2,1,0,3:T(4,128)S(1)}, ...), condition=%wide.region_5.6_spmd, body=%wide.region_2.5_spmd.sunk | while | flops 137632000 | bytes 7471827 | solution.py:153
  23.7 1.1 constant_dynamic-slice_fusion.3
  25.4 1.6 fusion.95
  28.5 1.1 constant_dynamic-slice_fusion.3
  30.2 1.6 fusion.95
  33.3 1.1 constant_dynamic-slice_fusion.3
  35.0 1.6 fusion.95
  39.8 1.6 fusion.95
  42.9 1.7 fusion.63
  46.1 1.1 collective-permute-done.3
  48.1 34.5 %all_to_all.36 = bf16[8,32,512]{2,1,0:T(8,128)(2,1)S(1)} all-to-all(bf16[8,32,512]{2,1,0:T(8,128)(2,1)S(1)} %copy.74), channel_id=1, replica_groups=mesh['req'=8,'tp'=4] {'req'}, dimensions={0} | all-to-all | bytes 524288 | tf_op jit(solution)/shard_map/all_to_all | solution.py:184
  83.5 14.9 %all-gather.8.cloned.1.call-done = bf16[8,128,512]{2,0,1:T(8,128)(2,1)} async-done(((bf16[8,32,512]{2,0,1:T(8,128)(2,1)}), bf16[8,128,512]{2,0,1:T(8,128)(2,1)}) %all-gather.8.cloned.1.call-update) | async-done | bytes 1048592 | tf_op jit(solution)/shard_map/all_gather | solution.py:185
  98.4 1.5 copy.76
  100.0 2.6 convolution_convert_fusion.3
  102.6 67.9 %reduce-scatter.5.cloned.1.call-done = bf16[128,1024]{1,0:T(8,128)(2,1)} async-done(((bf16[1024,1024]{1,0:T(8,128)(2,1)}), bf16[128,1024]{1,0:T(8,128)(2,1)}) %reduce-scatter.5.cloned.1.call-update) | async-done | bytes 262160 | tf_op jit(solution)/shard_map/reduce_scatter | solution.py:190
  170.6 3.4 all-to-all-start.1
  174.1 5.9 %all-to-all-done.1 = bf16[4,32,1024]{2,1,0:T(8,128)(2,1)S(1)} async-done(((bf16[4,32,1024]{2,1,0:T(8,128)(2,1)}), bf16[4,32,1024]{2,1,0:T(8,128)(2,1)S(1)}, u32[]{:S(2)}, u32[]{:S(2)}) %all-to-all-start.1) | async-done | bytes 262176 | tf_op jit(solution)/shard_map/all_to_all | solution.py:193
  180.6 12.1 %all_to_all.37 = bf16[8,32,512]{2,1,0:T(8,128)(2,1)S(1)} all-to-all(bf16[8,32,512]{2,1,0:T(8,128)(2,1)S(1)} %copy.78), channel_id=1, replica_groups=mesh['req'=8,'tp'=4] {'req'}, dimensions={0} | all-to-all | bytes 524288 | tf_op jit(solution)/shard_map/all_to_all | solution.py:184
  193.9 14.8 %all-gather.10.cloned.1.call-done = bf16[8,128,512]{2,0,1:T(8,128)(2,1)} async-done(((bf16[8,32,512]{2,0,1:T(8,128)(2,1)}), bf16[8,128,512]{2,0,1:T(8,128)(2,1)}) %all-gather.10.cloned.1.call-update) | async-done | bytes 1048592 | tf_op jit(solution)/shard_map/all_gather | solution.py:185
  208.6 1.5 copy.80
  210.2 3.4 convolution_convert_fusion
  213.7 4.9 %convolution_convert_fusion.1 = bf16[1024,1536]{1,0:T(8,128)(2,1)} fusion(bf16[1024,512]{1,0:T(8,128)(2,1)S(1)} %bitcast.175, bf16[512,1536]{1,0:T(8,128)(2,1)} %param.31), kind=kOutput, calls=%fused_computation.17 | convolution fusion | flops 1612185600 | bytes 5767168 | tf_op jit(solution)/shard_map/dot_general | solution.py:203
  218.7 69.6 %reduce-scatter.9.cloned.1.call-done = bf16[128,1536]{1,0:T(8,128)(2,1)} async-done(((bf16[1024,1536]{1,0:T(8,128)(2,1)}), bf16[128,1536]{1,0:T(8,128)(2,1)}) %reduce-scatter.9.cloned.1.call-update) | async-done | bytes 393232 | tf_op jit(solution)/shard_map/reduce_scatter | solution.py:208
  288.2 77.0 %reduce-scatter.7.cloned.1.call-done = bf16[128,1536]{1,0:T(8,128)(2,1)} async-done(((bf16[1024,1536]{1,0:T(8,128)(2,1)}), bf16[128,1536]{1,0:T(8,128)(2,1)}) %reduce-scatter.7.cloned.1.call-update) | async-done | bytes 393232 | tf_op jit(solution)/shard_map/reduce_scatter | solution.py:205
  365.3 2.1 fusion.11
  367.4 59.8 %all-gather.6.cloned.1.call-done = bf16[1024,1536]{1,0:T(8,128)(2,1)} async-done(((bf16[128,1536]{1,0:T(8,128)(2,1)}), bf16[1024,1536]{1,0:T(8,128)(2,1)}) %all-gather.6.cloned.1.call-update) | async-done | bytes 3145744 | tf_op jit(solution)/shard_map/all_gather | solution.py:212
  427.2 3.7 convolution_convert_fusion.4
  433.6 22.1 %reduce-scatter.11.cloned.1.call-done = bf16[256,512]{1,0:T(8,128)(2,1)} async-done(((bf16[1024,512]{1,0:T(8,128)(2,1)}), bf16[256,512]{1,0:T(8,128)(2,1)}) %reduce-scatter.11.cloned.1.call-update) | async-done | bytes 262160 | tf_op jit(solution)/shard_map/reduce_scatter | solution.py:218
  455.7 5.5 %all-to-all-start.3 = ((bf16[8,32,512]{2,1,0:T(8,128)(2,1)}), bf16[8,32,512]{2,1,0:T(8,128)(2,1)S(1)}, u32[]{:S(2)}, u32[]{:S(2)}) async-start(bf16[8,32,512]{2,1,0:T(8,128)(2,1)} %bitcast.187), calls=%async_computation.7 | async-start | bytes 524288 | tf_op jit(solution)/shard_map/all_to_all | solution.py:219
  462.3 7.8 %all-to-all-done.3 = bf16[8,32,512]{2,1,0:T(8,128)(2,1)S(1)} async-done(((bf16[8,32,512]{2,1,0:T(8,128)(2,1)}), bf16[8,32,512]{2,1,0:T(8,128)(2,1)S(1)}, u32[]{:S(2)}, u32[]{:S(2)}) %all-to-all-start.3) | async-done | bytes 262176 | tf_op jit(solution)/shard_map/all_to_all | solution.py:219
  (153 shorter events, 28.4 us)
Async XLA Ops:
  7.2 203.0 %copy-start = (bf16[512,1536]{1,0:T(8,128)(2,1)S(1)}, bf16[512,1536]{1,0:T(8,128)(2,1)}, u32[]{:S(2)}) copy-start(bf16[512,1536]{1,0:T(8,128)(2,1)} %param.32) | copy-start | bytes 4718596
  7.2 2.4 copy-start.12
  7.2 91.2 %all-gather.8.cloned.1.call-start = ((), (), s32[]{:S(2)}) async-start(), calls=%async_computation.13 | async-start | bytes 1310720 | tf_op jit(solution)/shard_map/all_gather | solution.py:185
  12.6 2.0 copy-start.8
  12.9 1.8 copy-start.13
  13.9 8.5 %collective-permute-start = (bf16[32,4096]{1,0:T(8,128)(2,1)S(1)}, bf16[32,4096]{1,0:T(8,128)(2,1)S(1)}, u32[]{:S(2)}, u32[]{:S(2)}) collective-permute-start(bf16[32,4096]{1,0:T(8,128)(2,1)S(1)} %bitcast.186), channel_id=1, source_target_pairs={{0,1},{1,0},{2,3},{3,2},{4,5},{5,4},{6,7},{7,6},{8,9},{9,8},{10,11... | collective-permute-start | bytes 786440 | tf_op jit(solution)/shard_map/ppermute | solution.py:19
  16.0 3.7 copy-start.1
  19.7 1.9 copy-start.3
  22.6 0.9 copy-start.2
  44.7 1.4 collective-permute-start.1
  45.4 1.9 collective-permute-start.2
  46.1 1.2 collective-permute-start.3
  48.0 52.0 %copy-start.11 = (bf16[512,1024]{1,0:T(8,128)(2,1)S(1)}, bf16[512,1024]{1,0:T(8,128)(2,1)}, u32[]{:S(2)}) copy-start(bf16[512,1024]{1,0:T(8,128)(2,1)} %param.30) | copy-start | bytes 3145732
  83.5 87.1 %reduce-scatter.5.cloned.1.call-start = ((), (), s32[]{:S(2)}) async-start(), calls=%async_computation.8 | async-start | bytes 2359296 | tf_op jit(solution)/shard_map/reduce_scatter | solution.py:190
  102.6 71.4 %copy-start.9 = (bf16[4096]{0:T(1024)(128)(2,1)S(1)}, bf16[4096]{0:T(1024)(128)(2,1)}, u32[]{:S(2)}) copy-start(bf16[4096]{0:T(1024)(128)(2,1)} %param.29) | copy-start | bytes 24580
  102.6 77.5 %copy-start.7 = (bf16[32,4096]{1,0:T(8,128)(2,1)S(1)}, bf16[32,4096]{1,0:T(8,128)(2,1)}, u32[]{:S(2)}) copy-start(bf16[32,4096]{1,0:T(8,128)(2,1)} %param.18) | copy-start | bytes 786436
  170.6 9.4 %all-to-all-start.1 = ((bf16[4,32,1024]{2,1,0:T(8,128)(2,1)}), bf16[4,32,1024]{2,1,0:T(8,128)(2,1)S(1)}, u32[]{:S(2)}, u32[]{:S(2)}) async-start(bf16[4,32,1024]{2,1,0:T(8,128)(2,1)} %bitcast.188), calls=%async_computation.2 | async-start | bytes 524288 | tf_op jit(solution)/shard_map/all_to_all | solution.py:193
  174.0 34.7 %all-gather.10.cloned.1.call-start = ((), (), s32[]{:S(2)}) async-start(), calls=%async_computation.14 | async-start | bytes 1310720 | tf_op jit(solution)/shard_map/all_gather | solution.py:185
  193.6 94.6 %reduce-scatter.9.cloned.1.call-start = ((), (), s32[]{:S(2)}) async-start(), calls=%async_computation.10 | async-start | bytes 3538944 | tf_op jit(solution)/shard_map/reduce_scatter | solution.py:208
  213.7 151.6 %reduce-scatter.7.cloned.1.call-start = ((), (), s32[]{:S(2)}) async-start(), calls=%async_computation.9 | async-start | bytes 3538944 | tf_op jit(solution)/shard_map/reduce_scatter | solution.py:205
  218.6 208.6 %copy-start.10 = (bf16[1536,512]{1,0:T(8,128)(2,1)S(1)}, bf16[1536,512]{1,0:T(8,128)(2,1)}, u32[]{:S(2)}) copy-start(bf16[1536,512]{1,0:T(8,128)(2,1)} %param.33) | copy-start | bytes 4718596
  218.6 208.6 %all-gather.6.cloned.1.call-start = ((), (), s32[]{:S(2)}) async-start(), calls=%async_computation.11 | async-start | bytes 3538944 | tf_op jit(solution)/shard_map/all_gather | solution.py:212
  367.4 88.3 %reduce-scatter.11.cloned.1.call-start = ((), (), s32[]{:S(2)}) async-start(), calls=%async_computation.12 | async-start | bytes 1310720 | tf_op jit(solution)/shard_map/reduce_scatter | solution.py:218
  430.9 1.1 copy-start.5
  430.9 1.1 copy-start.6
  430.9 1.2 copy-start.4
  430.9 1.3 copy-start.14
  432.2 29.3 %collective-permute-start.4 = (bf16[32,2048]{1,0:T(8,128)(2,1)S(1)}, bf16[32,2048]{1,0:T(8,128)(2,1)S(1)}, u32[]{:S(2)}, u32[]{:S(2)}) collective-permute-start(bf16[32,2048]{1,0:T(8,128)(2,1)S(1)} %constant_dynamic-update-slice_fusion), channel_id=1, source_target_pairs={{0,1},{1,0},{2,3},{3,2},{4,5},{5,4},{6,7},{7,6},{8,9},{9,8},{10,11... | collective-permute-start | bytes 393224 | tf_op jit(solution)/shard_map/ppermute | solution.py:19
  455.7 14.4 %all-to-all-start.3 = ((bf16[8,32,512]{2,1,0:T(8,128)(2,1)}), bf16[8,32,512]{2,1,0:T(8,128)(2,1)S(1)}, u32[]{:S(2)}, u32[]{:S(2)}) async-start(bf16[8,32,512]{2,1,0:T(8,128)(2,1)} %bitcast.187), calls=%async_computation.7 | async-start | bytes 524288 | tf_op jit(solution)/shard_map/all_to_all | solution.py:219
Sparse Core Ops, SparseCore 0:
  83.6 14.7 all-gather.7
  102.7 67.7 reduce-scatter.4
  193.7 14.8 all-gather.9
  213.8 74.4 reduce-scatter.8
  291.7 73.5 reduce-scatter.6
  367.5 59.6 all-gather.5
  432.2 23.5 reduce-scatter.10

commit v2 on v1

--- a/solution.py
+++ b/solution.py
@@ -1,6 +1,10 @@
+import functools
+
 import jax
 import jax.numpy as jnp
 from jax import lax
+from jax.experimental import pallas as pl
+from jax.experimental.pallas import tpu as pltpu
 from jax.sharding import PartitionSpec as P
 
 HEADS = 32
@@ -37,6 +41,184 @@
         [front_half * cosine - back_half * sine_part, back_half * cosine + front_half * sine_part],
         axis=-1,
     )
+
+
+SIDE = 2
+MESH = pl.DeviceIdType.MESH
+ANY = pl.BlockSpec(memory_space=pl.ANY)
+
+
+def meet(peers):
+    barrier = pltpu.get_barrier_semaphore()
+    for peer in peers:
+        pl.semaphore_signal(barrier, inc=1, device_id=peer, device_id_type=MESH)
+    pl.semaphore_wait(barrier, len(peers))
+
+
+def remote(source, target, send_sem, recv_sem, peer):
+    return pltpu.make_async_remote_copy(
+        src_ref=source,
+        dst_ref=target,
+        send_sem=send_sem,
+        recv_sem=recv_sem,
+        device_id=peer,
+        device_id_type=MESH,
+    )
+
+
+def exchange_kernel(along, mode, rows_ref, out_ref, send_sem, recv_sem, own_sem):
+    tp_count = lax.axis_size("tp")
+    req, tp = lax.axis_index("req"), lax.axis_index("tp")
+    level, side = req // SIDE, req % SIDE
+    if along == "level":
+        count, mine = lax.axis_size("req") // SIDE, level
+    else:
+        count, mine = SIDE * tp_count, side * tp_count + tp
+
+    def device(index):
+        if along == "level":
+            return {"req": index * SIDE + side, "tp": tp}
+        return {"req": level * SIDE + index // tp_count, "tp": index % tp_count}
+
+    def part(index):
+        if mode == "copy":
+            return rows_ref
+        if mode == "inner":
+            return rows_ref.at[:, index]
+        return rows_ref.at[index]
+
+    others = [(mine + step) % count for step in range(1, count)]
+    meet([device(index) for index in others])
+    copies = [
+        remote(part(index), out_ref.at[mine], send_sem.at[at], recv_sem.at[at], device(index))
+        for at, index in enumerate(others)
+    ]
+    for copy in copies:
+        copy.start()
+    own = pltpu.make_async_copy(part(mine), out_ref.at[mine], own_sem)
+    own.start()
+    for copy in copies:
+        copy.wait()
+    own.wait()
+
+
+def exchange(rows, along, mode, collective_id):
+    count = lax.axis_size("req") // SIDE if along == "level" else SIDE * lax.axis_size("tp")
+    if mode == "copy":
+        part_shape = rows.shape
+    elif mode == "inner":
+        part_shape = rows.shape[:1] + rows.shape[2:]
+    else:
+        part_shape = rows.shape[1:]
+    return pl.pallas_call(
+        functools.partial(exchange_kernel, along, mode),
+        out_shape=jax.ShapeDtypeStruct((count, *part_shape), rows.dtype),
+        in_specs=[ANY],
+        out_specs=ANY,
+        scratch_shapes=[
+            pltpu.SemaphoreType.DMA((count - 1,)),
+            pltpu.SemaphoreType.DMA((count - 1,)),
+            pltpu.SemaphoreType.DMA,
+        ],
+        compiler_params=pltpu.CompilerParams(collective_id=collective_id, has_side_effects=True),
+    )(rows)
+
+
+def slices_kernel(
+    rows_ref, out_ref, send_level, recv_level, send_far, recv_far, send_core, recv_core, own_sem
+):
+    tp_count = lax.axis_size("tp")
+    levels = lax.axis_size("req") // SIDE
+    req, tp = lax.axis_index("req"), lax.axis_index("tp")
+    level, side = req // SIDE, req % SIDE
+    place = side * tp_count + tp
+    core, chip = tp % 2, place // 2
+    chips = SIDE * tp_count // 2
+    width = rows_ref.shape[1] // levels
+
+    def columns(index):
+        return rows_ref.at[:, pl.ds(pl.multiple_of(index * width, width), width)]
+
+    def chip_place(index):
+        return index * 2 + core
+
+    def device(at):
+        return {"req": level * SIDE + at // tp_count, "tp": at % tp_count}
+
+    level_ids = [(level + step) % levels for step in range(1, levels)]
+    level_devices = [{"req": index * SIDE + side, "tp": tp} for index in level_ids]
+    far_devices = [device(chip_place((chip + step) % chips)) for step in range(1, chips)]
+    core_device = device(chip * 2 + 1 - core)
+    meet(level_devices + far_devices + [core_device])
+    first = [
+        remote(columns(index), out_ref.at[level, place], send_level.at[at], recv_level.at[at], peer)
+        for at, (index, peer) in enumerate(zip(level_ids, level_devices))
+    ]
+    for copy in first:
+        copy.start()
+    own = pltpu.make_async_copy(columns(level), out_ref.at[level, place], own_sem)
+    own.start()
+    for copy in first:
+        copy.wait()
+    own.wait()
+    mine = out_ref.at[:, place]
+    far = [
+        remote(mine, mine, send_far.at[at], recv_far.at[at], peer)
+        for at, peer in enumerate(far_devices)
+    ]
+    for copy in far:
+        copy.start()
+    near = [remote(mine, mine, send_core.at[0], recv_core.at[0], core_device)]
+    near[0].start()
+    for step in range(1, chips):
+        far[step - 1].wait_recv()
+        landed = out_ref.at[:, chip_place((chip - step + chips) % chips)]
+        copy = remote(landed, landed, send_core.at[step], recv_core.at[step], core_device)
+        copy.start()
+        near.append(copy)
+    for copy in near:
+        copy.wait()
+    for copy in far:
+        copy.wait_send()
+
+
+def feature_slices(rows, collective_id):
+    levels = lax.axis_size("req") // SIDE
+    places = SIDE * lax.axis_size("tp")
+    width = rows.shape[1] // levels
+    chips = places // 2
+    gathered = pl.pallas_call(
+        slices_kernel,
+        out_shape=jax.ShapeDtypeStruct((levels, places, rows.shape[0], width), rows.dtype),
+        in_specs=[ANY],
+        out_specs=ANY,
+        scratch_shapes=[
+            pltpu.SemaphoreType.DMA((levels - 1,)),
+            pltpu.SemaphoreType.DMA((levels - 1,)),
+            pltpu.SemaphoreType.DMA((chips - 1,)),
+            pltpu.SemaphoreType.DMA((chips - 1,)),
+            pltpu.SemaphoreType.DMA((chips,)),
+            pltpu.SemaphoreType.DMA((chips,)),
+            pltpu.SemaphoreType.DMA,
+        ],
+        compiler_params=pltpu.CompilerParams(collective_id=collective_id, has_side_effects=True),
+    )(rows)
+    return gathered.reshape(-1, width)
+
+
+def paired_halves(shard, axis):
+    side = lax.axis_index("req") % SIDE
+    half = shard.shape[axis] // 2
+    kept = lax.dynamic_slice_in_dim(shard, side * half, half, axis)
+    sent = lax.dynamic_slice_in_dim(shard, (1 - side) * half, half, axis)
+    return kept, sent
+
+
+def joined(kept, received, axis):
+    side = lax.axis_index("req") % SIDE
+    low = jnp.where(side == 0, kept, received)
+    high = jnp.where(side == 0, received, kept)
+    return jnp.concatenate([low, high], axis=axis)
 
 
 def ancestors(parent_row):
@@ -71,6 +253,17 @@
     down_weight,
 ):
     half_rows = queries.shape[0]
+    out_kept, out_sent = paired_halves(out_weight, 1)
+    out_received = swapped(out_sent, "req", 0)
+    gate_kept, gate_sent = paired_halves(gate_weight, 1)
+    up_kept, up_sent = paired_halves(up_weight, 1)
+    gate_up_received = swapped(jnp.concatenate([gate_sent, up_sent], axis=1), "req", 0)
+    gate_up_kept = jnp.concatenate([gate_kept, up_kept], axis=1)
+    down_kept, down_sent = paired_halves(down_weight, 0)
+    down_received = swapped(down_sent, "req", 0)
+    out_full = joined(out_kept, out_received, 0)
+    gate_up_full = joined(gate_up_kept, gate_up_received, 0)
+    down_full = joined(down_kept, down_received, 1)
     tree_size = 2 * half_rows
     group_size = HEADS // KV_HEADS
     kv_width = new_keys.shape[1]
@@ -176,49 +369,38 @@
     accepted_kv = jnp.dot(
         chosen.astype(jnp.bfloat16), fresh_all, preferred_element_type=jnp.float32
     ).astype(jnp.bfloat16)
-    req_count = lax.axis_size("req")
-
-    def feature_slices(rows):
-        parts = rows.reshape(half_rows, req_count, -1)
-        parts = jnp.transpose(parts, (1, 0, 2))
-        parts = lax.all_to_all(parts, "req", split_axis=0, concat_axis=0, tiled=True)
-        parts = lax.all_gather(parts[:, None], "tp", axis=1, tiled=True)
-        return parts.reshape(req_count * tp_count * half_rows, -1)
-
-    attn_slice = feature_slices(attended)
-    projected = jnp.dot(attn_slice, out_weight, preferred_element_type=jnp.float32)
-    projected = lax.psum_scatter(
-        projected.astype(jnp.bfloat16), "req", scatter_dimension=0, tiled=True
-    )
-    own_projected = lax.all_to_all(
-        projected, "tp", split_axis=0, concat_axis=1, tiled=True
-    ).astype(jnp.float32)
-    residual = (hidden_in.astype(jnp.float32) + own_projected).astype(jnp.bfloat16)
+    levels = lax.axis_size("req") // SIDE
+    places = SIDE * tp_count
+    attn_slice = feature_slices(attended, 0)
+    projected = jnp.dot(attn_slice, out_full, preferred_element_type=jnp.float32)
+    projected = projected.astype(jnp.bfloat16).reshape(levels, places * half_rows, -1)
+    projected = exchange(projected, "level", "lead", 1)
+    projected = jnp.sum(projected.astype(jnp.float32), axis=0).astype(jnp.bfloat16)
+    projected = exchange(projected.reshape(places, half_rows, -1), "place", "lead", 2)
+    own_projected = jnp.transpose(
+        projected.reshape(SIDE, tp_count, half_rows, -1), (2, 1, 0, 3)
+    ).reshape(half_rows, -1)
+    residual = (hidden_in.astype(jnp.float32) + own_projected.astype(jnp.float32)).astype(
+        jnp.bfloat16
+    )
     residual_wide = residual.astype(jnp.float32)
     mean_sq = jnp.mean(residual_wide * residual_wide, axis=-1, keepdims=True)
     normed = (residual_wide * lax.rsqrt(mean_sq + EPS) * post_gain.astype(jnp.float32)).astype(
         jnp.bfloat16
     )
-    normed_slice = feature_slices(normed)
-    gate_part = jnp.dot(normed_slice, gate_weight, preferred_element_type=jnp.float32)
-    up_part = jnp.dot(normed_slice, up_weight, preferred_element_type=jnp.float32)
-    gate_sum = lax.psum_scatter(
-        gate_part.astype(jnp.bfloat16), "req", scatter_dimension=0, tiled=True
-    ).astype(jnp.float32)
-    up_sum = lax.psum_scatter(
-        up_part.astype(jnp.bfloat16), "req", scatter_dimension=0, tiled=True
-    ).astype(jnp.float32)
-    hidden = (jax.nn.silu(gate_sum) * up_sum).astype(jnp.bfloat16)
-    hidden_all = lax.all_gather(hidden, "req", axis=0, tiled=True)
-    partial_out = jnp.dot(hidden_all, down_weight, preferred_element_type=jnp.float32)
-    partial_out = partial_out.astype(jnp.bfloat16).reshape(req_count, tp_count, half_rows, -1)
-    partial_out = jnp.transpose(partial_out, (1, 0, 2, 3)).reshape(
-        tp_count * req_count * half_rows, -1
-    )
-    paired_sum = lax.psum_scatter(partial_out, "tp", scatter_dimension=0, tiled=True)
-    mlp_own = lax.all_to_all(
-        paired_sum, "req", split_axis=0, concat_axis=1, tiled=True
-    ).astype(jnp.float32)
+    normed_slice = feature_slices(normed, 3)
+    sums = jnp.dot(normed_slice, gate_up_full, preferred_element_type=jnp.float32)
+    sums = sums.astype(jnp.bfloat16).reshape(levels, places * half_rows, -1)
+    sums = jnp.sum(exchange(sums, "level", "lead", 4).astype(jnp.float32), axis=0)
+    hidden_width = sums.shape[1] // 2
+    hidden = (jax.nn.silu(sums[:, :hidden_width]) * sums[:, hidden_width:]).astype(jnp.bfloat16)
+    hidden_all = exchange(hidden, "level", "copy", 5).reshape(-1, hidden_width)
+    partial_out = jnp.dot(hidden_all, down_full, preferred_element_type=jnp.float32)
+    partial_out = partial_out.astype(jnp.bfloat16).reshape(levels, places, half_rows, -1)
+    paired_sum = exchange(partial_out, "place", "inner", 6).astype(jnp.float32)
+    paired_sum = jnp.sum(paired_sum, axis=0).astype(jnp.bfloat16)
+    mlp_own = exchange(paired_sum, "level", "lead", 7)
+    mlp_own = jnp.transpose(mlp_own, (1, 0, 2)).reshape(half_rows, -1).astype(jnp.float32)
     layer_out = (residual_wide + mlp_own).astype(jnp.bfloat16)
     return (layer_out, accepted_kv)
 

time: 480 us -> 329 us (0.69)
  waiting for transfers between devices: 341 us -> 0.03 us
  Pallas kernels: 0 us -> 250 us
  blocking collectives: 46.7 us -> 0 us
  between operations: 16.1 us -> 2.71 us
  other arithmetic: 14.2 us -> 27.5 us
  matrix products: 29.6 us -> 22 us
  starting transfers between devices: 10.6 us -> 5.57 us
    pallas_call x0 -> x8, Pallas kernels: none -> 250 us  [the longest x6 177 us: exchange(): pl.pallas_call(functools.partial(exchange_kernel, along, mode), out_shape...]
    reduce_scatter x4 -> x0, waiting for transfers between devices: 237 us -> none  [the longest x1 77 us: per_device(): lax.psum_scatter(gate_part.astype(jnp.bfloat16), 'req', scatter_dimension...]
    all_gather x3 -> x0, waiting for transfers between devices: 89.5 us -> none  [the longest x1 59.8 us: per_device(): hidden_all = lax.all_gather(hidden, 'req', axis=0, tiled=True)]
    all_to_all x2 -> x0, blocking collectives: 46.7 us -> none  [feature_slices(): lax.all_to_all(parts, 'req', split_axis=0, concat_axis=0, tiled=True)]
    all_to_all x2 -> x0, waiting for transfers between devices: 13.8 us -> none  [the longest x1 7.84 us: per_device(): lax.all_to_all(paired_sum, 'req', split_axis=0, concat_axis=1, tiled=True)]
    all_to_all x2 -> x0, starting transfers between devices: 8.91 us -> none  [the longest x1 5.51 us: per_device(): lax.all_to_all(paired_sum, 'req', split_axis=0, concat_axis=1, tiled=True)]
    reduce_sum x0 -> x3, other arithmetic: none -> 7.48 us  [the longest x1 2.73 us: per_device(): paired_sum = jnp.sum(paired_sum, axis=0).astype(jnp.bfloat16)]
    select_n x0 -> x3, other arithmetic: none -> 6.3 us  [joined(): low = jnp.where(side == 0, kept, received)]
  transfers between devices with their start and end apart: 14 -> 8, of which waited for: 10 -> 0; matrix products, arithmetic and copies ran while one was open for 3% -> 13% of each run, Pallas kernels for 0% -> 33%
where the time goes in v2:
time: 329 us; the launch traced here: 328 us
  Pallas kernels  250 us (76%)
  other arithmetic  27.5 us (8%)
  matrix products  22 us (7%)
  local copies, waits for them, and re-layouts  19.9 us (6%)
  starting transfers between devices  5.57 us (2%)
    pallas_call x6, Pallas kernels, exchange(): pl.pallas_call(functools.partial(exchange_kernel, along, mode), out_shape...  177 us
    pallas_call x2, Pallas kernels, feature_slices(): pl.pallas_call(slices_kernel, out_shape=jax.ShapeDtypeStruct((levels, pla...  73 us
    unnamed x50, local copies, waits for them, and re-layouts  7.03 us
  transfers between devices with their start and end apart: 8, of which 0 were waited for; matrix products, arithmetic and copies ran while one was open for 13% of the time, Pallas kernels for 33%

profile of v2, /device:TPU:0, one launch (start us, length us, event | category | flops | bytes accessed | tf_op | source)
XLA Modules:
  0.0 328.1 jit_solution(5984891032129692285)
XLA Ops:
  8.5 2.5 collective-permute-start.4
  11.0 2.5 constant_dynamic-slice_fusion.5
  13.5 1.3 pad_maximum_fusion.1
  18.7 1.0 constant_dynamic-slice_fusion.2
  20.5 3.7 %copy.68 = bf16[128,8,8,128]{3,2,1,0:T(8,128)(2,1)} copy(bf16[128,8,8,128]{3,1,2,0:T(8,128)(2,1)} %bitcast.157) | data formatting | bytes 4194304
  24.2 1.9 copy.71
  26.9 11.5 %while.14 = (s32[]{:T(128)}, f32[8,4,64,1]{2,1,0,3:T(4,128)S(1)}, f32[8,4,64,1]{2,1,0,3:T(4,128)S(1)}, f32[8,4,64,128]{3,2,1,0:T(8,128)S(1)}, s32[]{:T(128)}, /*...) while((s32[]{:T(128)}, f32[8,4,64,1]{2,1,0,3:T(4,128)S(1)}, ...), condition=%wide.region_5.6_spmd, body=%wide.region_2.5_spmd.sunk | while | flops 137632000 | bytes 7471827 | solution.py:346
  26.9 1.1 constant_dynamic-slice_fusion.10
  30.7 1.1 constant_dynamic-slice_fusion.10
  34.4 1.1 constant_dynamic-slice_fusion.10
  38.4 1.5 fusion.72
  41.4 1.8 convolution_convert_fusion.1
  43.2 1.8 collective-permute-start.6
  46.6 43.5 %shard_map.167 = bf16[4,8,32,1024]{3,2,1,0:T(8,128)(2,1)} custom-call(bf16[32,4096]{1,0:T(8,128)(2,1)} %convert_element_type.156.rows_ref), custom_call_target="tpu_custom_call" | custom-call | tf_op jit(solution)/shard_map/pallas_call | solution.py:190
  90.1 1.4 broadcast_select_fusion.5
  91.9 2.2 convolution_convert_fusion.3
  94.1 23.3 %shard_map.168 = bf16[4,256,512]{2,1,0:T(8,128)(2,1)} custom-call(bf16[4,256,512]{2,1,0:T(8,128)(2,1)} %bitcast.165), custom_call_target="tpu_custom_call" | custom-call | tf_op jit(solution)/shard_map/pallas_call | solution.py:113
  117.5 2.2 reduce_sum.91
  119.7 10.3 %shard_map.169 = bf16[8,32,512]{2,1,0:T(8,128)(2,1)} custom-call(bf16[8,32,512]{2,1,0:T(8,128)(2,1)} %bitcast.163), custom_call_target="tpu_custom_call" | custom-call | tf_op jit(solution)/shard_map/pallas_call | solution.py:113
  130.0 1.2 copy.86
  132.7 29.4 %shard_map.170 = bf16[4,8,32,1024]{3,2,1,0:T(8,128)(2,1)} custom-call(bf16[32,4096]{1,0:T(8,128)(2,1)} %fusion.19.rows_ref), custom_call_target="tpu_custom_call" | custom-call | tf_op jit(solution)/shard_map/pallas_call | solution.py:190
  162.2 2.7 broadcast_select_fusion.3
  164.9 2.2 broadcast_select_fusion.1
  167.1 4.9 %convolution_convert_fusion = bf16[1024,1536]{1,0:T(8,128)(2,1)} fusion(bf16[1024,1024]{1,0:T(8,128)(2,1)S(1)} %bitcast.155, bf16[512,1536]{1,0:T(8,128)(2,1)S(1)} %get-tuple-element.121, bf16[512,1536]{1,0:T(8,128)(2,1)S(1)} %get-tuple-element.120), kind=kOutput, calls=%fused_computation.17 | convolution fusion | flops 3229089792 | bytes 8388608 | tf_op jit(solution)/shard_map/dot_general | solution.py:392
  172.0 55.8 %shard_map.171 = bf16[4,256,1536]{2,1,0:T(8,128)(2,1)} custom-call(bf16[4,256,1536]{2,1,0:T(8,128)(2,1)} %bitcast.153), custom_call_target="tpu_custom_call" | custom-call | tf_op jit(solution)/shard_map/pallas_call | solution.py:113
  227.8 2.6 convert_reduce_fusion.1
  231.3 45.2 %shard_map.172 = bf16[4,256,768]{2,1,0:T(8,128)(2,1)} custom-call(bf16[256,768]{1,0:T(8,128)(2,1)} %fusion.16.rows_ref), custom_call_target="tpu_custom_call" | custom-call | tf_op jit(solution)/shard_map/pallas_call | solution.py:113
  276.5 4.5 %convolution_convert_fusion.2 = bf16[1024,1024]{1,0:T(8,128)(2,1)} fusion(bf16[1024,768]{1,0:T(8,128)(2,1)} %bitcast.162, bf16[768,512]{1,0:T(8,128)(2,1)S(1)} %copy-done.11, bf16[768,512]{1,0:T(8,128)(2,1)S(1)} %copy-done.10), kind=kOutput, calls=%fused_computation.22 | convolution fusion | flops 1614807040 | bytes 5242880 | tf_op jit(solution)/shard_map/dot_general | solution.py:398
  281.0 25.8 %shard_map.173 = bf16[8,4,32,1024]{3,2,1,0:T(8,128)(2,1)} custom-call(bf16[4,8,32,1024]{3,2,1,0:T(8,128)(2,1)} %bitcast.159), custom_call_target="tpu_custom_call" | custom-call | tf_op jit(solution)/shard_map/pallas_call | solution.py:113
  306.9 2.7 reduce_sum.94.rows_ref
  309.6 16.6 %shard_map.174 = bf16[4,32,1024]{2,1,0:T(8,128)(2,1)} custom-call(bf16[4,32,1024]{2,1,0:T(8,128)(2,1)} %reduce_sum.94.rows_ref), custom_call_target="tpu_custom_call" | custom-call | tf_op jit(solution)/shard_map/pallas_call | solution.py:113
  326.3 1.0 convert_bitcast_fusion
  (148 shorter events, 26.1 us)
Async XLA Ops:
  0.6 3.5 %copy-start = (s32[16,64]{1,0:T(8,128)S(1)}, s32[16,64]{1,0:T(8,128)}, u32[]{:S(2)}) copy-start(s32[16,64]{1,0:T(8,128)} %param.25) | copy-start | bytes 12292
  0.6 2.2 copy-start.19
  5.2 2.5 copy-start.8
  5.7 5.3 %copy-start.7 = (bf16[512,1536]{1,0:T(8,128)(2,1)S(1)}, bf16[512,1536]{1,0:T(8,128)(2,1)}, u32[]{:S(2)}) copy-start(bf16[512,1536]{1,0:T(8,128)(2,1)} %param.32) | copy-start | bytes 4718596
  7.2 19.1 %collective-permute-start = (bf16[32,4096]{1,0:T(8,128)(2,1)}, bf16[32,4096]{1,0:T(8,128)(2,1)S(1)}, u32[]{:S(2)}, u32[]{:S(2)}) collective-permute-start(bf16[32,4096]{1,0:T(8,128)(2,1)} %bitcast.135), channel_id=1, source_target_pairs={{0,1},{1,0},{2,3},{3,2},{4,5},{5,4},{6,7},{7,6},{8,9},{9,8},{10,11... | collective-permute-start | bytes 786440 | tf_op jit(solution)/shard_map/ppermute | solution.py:23
  8.5 81.6 %collective-permute-start.4 = (bf16[512,512]{1,0:T(8,128)(2,1)}, bf16[512,512]{1,0:T(8,128)(2,1)}, u32[]{:S(2)}, u32[]{:S(2)}) collective-permute-start(bf16[512,512]{1,0:T(8,128)(2,1)} %constant_dynamic-slice_fusion.7), channel_id=1, source_target_pairs={{0,4},{4,0},{8,12},{12,8},{16,20},{20,16},{24,28},{28,24},{1,5},{5... | collective-permute-start | bytes 1572872 | tf_op jit(solution)/shard_map/ppermute | solution.py:23
  13.5 1.4 copy-start.17
  13.5 1.4 copy-start.20
  13.5 2.6 copy-start.12
  13.5 3.7 %copy-start.21 = (s32[16]{0:T(128)S(1)}, s32[16]{0:T(128)}, u32[]{:S(2)}) copy-start(s32[16]{0:T(128)} %param.26) | copy-start | bytes 196
  13.5 5.1 %copy-start.5 = (bf16[1536,512]{1,0:T(8,128)(2,1)S(1)}, bf16[1536,512]{1,0:T(8,128)(2,1)}, u32[]{:S(2)}) copy-start(bf16[1536,512]{1,0:T(8,128)(2,1)} %param.33) | copy-start | bytes 4718596
  14.8 150.1 %collective-permute-start.5 = (bf16[512,1536]{1,0:T(8,128)(2,1)}, bf16[512,1536]{1,0:T(8,128)(2,1)}, u32[]{:S(2)}, u32[]{:S(2)}) collective-permute-start(bf16[512,1536]{1,0:T(8,128)(2,1)} %pad_maximum_fusion.1), channel_id=1, source_target_pairs={{0,4},{4,0},{8,12},{12,8},{16,20},{20,16},{24,28},{28,24},{1,5},{5... | collective-permute-start | bytes 4718600 | tf_op jit(solution)/shard_map/ppermute | solution.py:23
  15.4 8.8 %copy-start.14 = (bf16[32,8,64]{2,0,1:T(8,128)(2,1)}, bf16[32,8,64]{2,0,1:T(8,128)(2,1)S(1)}, u32[]{:S(2)}) copy-start(bf16[32,8,64]{2,0,1:T(8,128)(2,1)S(1)} %get-tuple-element.132) | copy-start | bytes 98308
  15.4 8.8 %copy-start.15 = (bf16[32,8,64]{2,0,1:T(8,128)(2,1)}, bf16[32,8,64]{2,0,1:T(8,128)(2,1)S(1)}, u32[]{:S(2)}) copy-start(bf16[32,8,64]{2,0,1:T(8,128)(2,1)S(1)} %get-tuple-element.133) | copy-start | bytes 98308
  16.7 24.6 %collective-permute-start.7 = (bf16[32,2048]{1,0:T(8,128)(2,1)}, bf16[32,2048]{1,0:T(8,128)(2,1)}, u32[]{:S(2)}, u32[]{:S(2)}) collective-permute-start(bf16[32,2048]{1,0:T(8,128)(2,1)} %constant_dynamic-update-slice_fusion), channel_id=1, source_target_pairs={{0,1},{1,0},{2,3},{3,2},{4,5},{5,4},{6,7},{7,6},{8,9},{9,8},{10,11... | collective-permute-start | bytes 393224 | tf_op jit(solution)/shard_map/ppermute | solution.py:23
  20.5 3.7 %copy-start.4 = (bf16[1024,1024]{1,0:T(8,128)(2,1)S(1)}, bf16[1024,1024]{1,0:T(8,128)(2,1)}, u32[]{:S(2)}) copy-start(bf16[1024,1024]{1,0:T(8,128)(2,1)} %param.23) | copy-start | bytes 6291460
  24.2 2.0 copy-start.13
  24.2 2.0 copy-start.18
  40.0 3.2 collective-permute-start.1
  40.3 4.7 %collective-permute-start.3 = (bf16[8,4,32,1]{2,1,0,3:T(4,128)(2,1)S(1)}, bf16[8,4,32,1]{2,1,0,3:T(4,128)(2,1)S(1)}, u32[]{:S(2)}, u32[]{:S(2)}) collective-permute-start(bf16[8,4,32,1]{2,1,0,3:T(4,128)(2,1)S(1)} %slice.113), channel_id=1, source_target_pairs={{0,1},{1,0},{2,3},{3,2},{4,5},{5,4},{6,7},{7,6},{8,9},{9,8},{10,11... | collective-permute-start | bytes 6152 | tf_op jit(solution)/shard_map/ppermute | solution.py:23
  41.4 3.7 %collective-permute-start.2 = (bf16[8,4,32,128]{3,2,1,0:T(8,128)(2,1)S(1)}, bf16[8,4,32,128]{3,2,1,0:T(8,128)(2,1)S(1)}, u32[]{:S(2)}, u32[]{:S(2)}) collective-permute-start(bf16[8,4,32,128]{3,2,1,0:T(8,128)(2,1)S(1)} %slice.112), channel_id=1, source_target_pairs={{0,1},{1,0},{2,3},{3,2},{4,5},{5,4},{6,7},{7,6},{8,9},{9,8},{10,11... | collective-permute-start | bytes 786440 | tf_op jit(solution)/shard_map/ppermute | solution.py:23
  43.2 118.9 %collective-permute-start.6 = (bf16[768,512]{1,0:T(8,128)(2,1)}, bf16[768,512]{1,0:T(8,128)(2,1)}, u32[]{:S(2)}, u32[]{:S(2)}) collective-permute-start(bf16[768,512]{1,0:T(8,128)(2,1)} %constant_dynamic-slice_fusion.2), channel_id=1, source_target_pairs={{0,4},{4,0},{8,12},{12,8},{16,20},{20,16},{24,28},{28,24},{1,5},{5... | collective-permute-start | bytes 2359304 | tf_op jit(solution)/shard_map/ppermute | solution.py:23
  45.0 45.1 %copy-start.9 = (bf16[512,1024]{1,0:T(8,128)(2,1)S(1)}, bf16[512,1024]{1,0:T(8,128)(2,1)}, u32[]{:S(2)}) copy-start(bf16[512,1024]{1,0:T(8,128)(2,1)} %param.30) | copy-start | bytes 3145732
  90.1 1.7 copy-start.3
  117.4 14.2 %copy-start.16 = (bf16[32,4096]{1,0:T(8,128)(2,1)S(1)}, bf16[32,4096]{1,0:T(8,128)(2,1)}, u32[]{:S(2)}) copy-start(bf16[32,4096]{1,0:T(8,128)(2,1)} %param.18) | copy-start | bytes 786436
  131.9 30.3 %copy-start.6 = (bf16[1536,512]{1,0:T(8,128)(2,1)S(1)}, bf16[1536,512]{1,0:T(8,128)(2,1)}, u32[]{:S(2)}) copy-start(bf16[1536,512]{1,0:T(8,128)(2,1)} %param.33) | copy-start | bytes 4718596
  162.2 2.8 copy-start.1
  164.9 2.2 copy-start.2
  230.3 46.2 %copy-start.10 = (bf16[768,512]{1,0:T(8,128)(2,1)S(1)}, bf16[768,512]{1,0:T(8,128)(2,1)}, u32[]{:S(2)}) copy-start(bf16[768,512]{1,0:T(8,128)(2,1)} %get-tuple-element.122) | copy-start | bytes 2359300
  230.3 46.2 %copy-start.11 = (bf16[768,512]{1,0:T(8,128)(2,1)S(1)}, bf16[768,512]{1,0:T(8,128)(2,1)}, u32[]{:S(2)}) copy-start(bf16[768,512]{1,0:T(8,128)(2,1)} %get-tuple-element.123) | copy-start | bytes 2359300

commit v3 on v2

--- a/solution.py
+++ b/solution.py
@@ -158,27 +158,35 @@
         copy.start()
     own = pltpu.make_async_copy(columns(level), out_ref.at[level, place], own_sem)
     own.start()
-    for copy in first:
-        copy.wait()
-    own.wait()
-    mine = out_ref.at[:, place]
-    far = [
-        remote(mine, mine, send_far.at[at], recv_far.at[at], peer)
-        for at, peer in enumerate(far_devices)
-    ]
-    for copy in far:
-        copy.start()
-    near = [remote(mine, mine, send_core.at[0], recv_core.at[0], core_device)]
-    near[0].start()
-    for step in range(1, chips):
-        far[step - 1].wait_recv()
-        landed = out_ref.at[:, chip_place((chip - step + chips) % chips)]
-        copy = remote(landed, landed, send_core.at[step], recv_core.at[step], core_device)
+    far, near = [], []
+    for step in range(levels):
+        source_level = (level - step + levels) % levels
+        target = out_ref.at[source_level, place]
+        if step > 0:
+            first[step - 1].wait_recv()
+        source = columns(level) if step == 0 else target
+        for peer in far_devices:
+            at = len(far)
+            copy = remote(source, target, send_far.at[at], recv_far.at[at], peer)
+            copy.start()
+            far.append(copy)
+        at = len(near)
+        copy = remote(source, target, send_core.at[at], recv_core.at[at], core_device)
         copy.start()
         near.append(copy)
+    for step in range(levels):
+        source_level = (level - step + levels) % levels
+        for hop in range(1, chips):
+            far[step * (chips - 1) + hop - 1].wait_recv()
+            landed = out_ref.at[source_level, chip_place((chip - hop + chips) % chips)]
+            at = len(near)
+            copy = remote(landed, landed, send_core.at[at], recv_core.at[at], core_device)
+            copy.start()
+            near.append(copy)
+    own.wait()
     for copy in near:
         copy.wait()
-    for copy in far:
+    for copy in first + far:
         copy.wait_send()
 
 
@@ -195,10 +203,10 @@
         scratch_shapes=[
             pltpu.SemaphoreType.DMA((levels - 1,)),
             pltpu.SemaphoreType.DMA((levels - 1,)),
-            pltpu.SemaphoreType.DMA((chips - 1,)),
-            pltpu.SemaphoreType.DMA((chips - 1,)),
-            pltpu.SemaphoreType.DMA((chips,)),
-            pltpu.SemaphoreType.DMA((chips,)),
+            pltpu.SemaphoreType.DMA((levels * (chips - 1),)),
+            pltpu.SemaphoreType.DMA((levels * (chips - 1),)),
+            pltpu.SemaphoreType.DMA((levels * chips,)),
+            pltpu.SemaphoreType.DMA((levels * chips,)),
             pltpu.SemaphoreType.DMA,
         ],
         compiler_params=pltpu.CompilerParams(collective_id=collective_id, has_side_effects=True),
@@ -219,6 +227,98 @@
     low = jnp.where(side == 0, kept, received)
     high = jnp.where(side == 0, received, kept)
     return jnp.concatenate([low, high], axis=axis)
+
+
+def attention_kernel(
+    limit_ref, query_ref, key_ref, value_ref, fresh_key_ref, fresh_value_ref, allowed_ref,
+    top_ref, total_ref, sum_ref,
+):
+    group_size = query_ref.shape[1] // HEAD_DIM
+    query = jnp.concatenate(
+        [query_ref[:, at * HEAD_DIM : (at + 1) * HEAD_DIM] for at in range(group_size)], axis=0
+    )
+    score_scale = HEAD_DIM ** (-0.5)
+    limit = limit_ref[0]
+    chunk = key_ref.shape[0] // 4
+
+    def score(keys):
+        return (
+            lax.dot_general(
+                query, keys, (((1,), (1,)), ((), ())), preferred_element_type=jnp.float32
+            )
+            * score_scale
+        )
+
+    def weigh(scores, top, allowed):
+        weights = jnp.where(allowed, jnp.exp(scores - top), 0.0).astype(jnp.bfloat16)
+        return weights, jnp.sum(weights.astype(jnp.float32), axis=-1, keepdims=True)
+
+    allowed = jnp.concatenate([allowed_ref[...]] * group_size, axis=0) > 0.5
+    scores = jnp.where(allowed, score(fresh_key_ref[...]), NEG)
+    top = jnp.max(scores, axis=-1, keepdims=True)
+    weights, total = weigh(scores, top, allowed)
+    summed = jnp.dot(weights, fresh_value_ref[...], preferred_element_type=jnp.float32)
+
+    def step(index, running):
+        top, total, summed = running
+        start = pl.multiple_of(index * chunk, chunk)
+        keys = key_ref[pl.ds(start, chunk), :]
+        values = value_ref[pl.ds(start, chunk), :]
+        allowed = lax.broadcasted_iota(jnp.int32, (query.shape[0], chunk), 1) + start < limit
+        scores = jnp.where(allowed, score(keys), NEG)
+        new_top = jnp.maximum(top, jnp.max(scores, axis=-1, keepdims=True))
+        weights, chunk_total = weigh(scores, new_top, allowed)
+        shrink = jnp.exp(top - new_top)
+        summed = summed * shrink + jnp.dot(weights, values, preferred_element_type=jnp.float32)
+        return new_top, total * shrink + chunk_total, summed
+
+    live = jnp.clip((limit + chunk - 1) // chunk, 0, 4)
+    top, total, summed = lax.fori_loop(0, live, step, (top, total, summed))
+    top_ref[0] = top
+    total_ref[0] = total
+    sum_ref[0] = summed
+
+
+def attend(limit, query, keys, values, fresh_keys, fresh_values, allowed):
+    rows, fresh_rows, cached_rows = query.shape[0], fresh_keys.shape[0], keys.shape[0]
+    group_size = HEADS // KV_HEADS
+    group_rows = rows * group_size
+
+    def columns(block_rows, width):
+        return pl.BlockSpec((block_rows, width), lambda head, limit_ref: (0, head))
+
+    def lead(width):
+        return pl.BlockSpec((1, group_rows, width), lambda head, limit_ref: (head, 0, 0))
+
+    results = pl.pallas_call(
+        attention_kernel,
+        out_shape=[
+            jax.ShapeDtypeStruct((KV_HEADS, group_rows, width), jnp.float32)
+            for width in (1, 1, HEAD_DIM)
+        ],
+        grid_spec=pltpu.PrefetchScalarGridSpec(
+            num_scalar_prefetch=1,
+            grid=(KV_HEADS,),
+            in_specs=[
+                columns(rows, group_size * HEAD_DIM),
+                columns(cached_rows, HEAD_DIM),
+                columns(cached_rows, HEAD_DIM),
+                columns(fresh_rows, HEAD_DIM),
+                columns(fresh_rows, HEAD_DIM),
+                pl.BlockSpec((rows, fresh_rows), lambda head, limit_ref: (0, 0)),
+            ],
+            out_specs=[lead(1), lead(1), lead(HEAD_DIM)],
+        ),
+        compiler_params=pltpu.CompilerParams(vmem_limit_bytes=32 * 2**20),
+        cost_estimate=pl.CostEstimate(
+            flops=4 * group_rows * cached_rows * KV_HEADS * HEAD_DIM,
+            bytes_accessed=4 * cached_rows * KV_HEADS * HEAD_DIM,
+            transcendentals=group_rows * cached_rows * KV_HEADS,
+        ),
+    )(limit, query, keys, values, fresh_keys, fresh_values, allowed)
+    return [
+        result.reshape(KV_HEADS, group_size, rows, result.shape[2]) for result in results
+    ]
 
 
 def ancestors(parent_row):
@@ -265,10 +365,8 @@
     gate_up_full = joined(gate_up_kept, gate_up_received, 0)
     down_full = joined(down_kept, down_received, 1)
     tree_size = 2 * half_rows
-    group_size = HEADS // KV_HEADS
     kv_width = new_keys.shape[1]
     q_width = queries.shape[1]
-    score_scale = HEAD_DIM ** (-0.5)
     tp_count = lax.axis_size("tp")
     device = lax.axis_index(("req", "tp"))
     request = device // 2
@@ -299,55 +397,17 @@
     query_own = query_heads.reshape(half_rows, q_width)
     fresh_own = jnp.concatenate([key_heads.reshape(half_rows, kv_width), new_values], axis=1)
     query_other, fresh_other = swapped((query_own, fresh_own), "tp", 0)
-    query_all = jnp.concatenate([query_own, query_other], axis=0).reshape(
-        tree_size, KV_HEADS, group_size, HEAD_DIM
-    )
-
-    def attend(running, block_keys, block_values, allowed):
-        run_top, run_total, summed = running
-        scores = (
-            jnp.einsum("qhgd,khd->hgqk", query_all, block_keys, preferred_element_type=jnp.float32)
-            * score_scale
-        )
-        scores = jnp.where(allowed, scores, NEG)
-        new_top = jnp.maximum(run_top, jnp.max(scores, axis=-1, keepdims=True))
-        weights = jnp.where(allowed, jnp.exp(scores - new_top), 0.0).astype(jnp.bfloat16)
-        shrink = jnp.exp(run_top - new_top)
-        run_total = run_total * shrink + jnp.sum(
-            weights.astype(jnp.float32), axis=-1, keepdims=True
-        )
-        summed = summed * shrink + jnp.einsum(
-            "hgqk,khd->hgqd", weights, block_values, preferred_element_type=jnp.float32
-        )
-        return (new_top, run_total, summed)
-
-    shard_rows = key_cache.shape[0]
-    block_rows = shard_rows // 8
-    key_blocks = key_cache.reshape(8, block_rows, KV_HEADS, HEAD_DIM)
-    value_blocks = value_cache.reshape(8, block_rows, KV_HEADS, HEAD_DIM)
-    first_block = pair_side * 8
-    stride = 1
-    needed = (cache_length + block_rows - 1) // block_rows
-    live_blocks = jnp.clip((needed - first_block + stride - 1) // stride, 0, 8)
-
-    def cache_step(block_index, running):
-        block_keys = lax.dynamic_index_in_dim(key_blocks, block_index, 0, keepdims=False)
-        block_values = lax.dynamic_index_in_dim(value_blocks, block_index, 0, keepdims=False)
-        first_slot = (first_block + stride * block_index) * block_rows
-        allowed = first_slot + jnp.arange(block_rows, dtype=jnp.int32) < cache_length
-        allowed = jnp.broadcast_to(allowed[None, :], (tree_size, block_rows))
-        return attend(running, block_keys, block_values, allowed)
-
-    initial = (
-        jnp.full((KV_HEADS, group_size, tree_size, 1), NEG, jnp.float32),
-        jnp.zeros((KV_HEADS, group_size, tree_size, 1), jnp.float32),
-        jnp.zeros((KV_HEADS, group_size, tree_size, HEAD_DIM), jnp.float32),
-    )
-    running = lax.fori_loop(0, live_blocks, cache_step, initial)
-    running = attend(
-        running, key_heads, new_values.reshape(half_rows, KV_HEADS, HEAD_DIM), own_cols
-    )
-    run_top, run_total, summed = running
+    query_all = jnp.concatenate([query_own, query_other], axis=0)
+    limit = (cache_length - pair_side * key_cache.shape[0]).reshape(1)
+    run_top, run_total, summed = attend(
+        limit,
+        query_all,
+        key_cache,
+        value_cache,
+        key_heads.reshape(half_rows, kv_width),
+        new_values,
+        own_cols.astype(jnp.float32),
+    )
     far_top, far_total, far_sum = (
         swapped(run_top[:, :, half_rows:].astype(jnp.bfloat16), "tp", 0).astype(jnp.float32),
         swapped(run_total[:, :, half_rows:].astype(jnp.bfloat16), "tp", 0).astype(jnp.float32),

time: 329 us -> 313 us (0.951)
  matrix products: 22 us -> 16.2 us
  other arithmetic: 27.5 us -> 23.9 us
    pallas_call x0 -> x1, Pallas kernels: none -> 19 us  [attend(): pl.pallas_call(attention_kernel, out_shape=[jax.ShapeDtypeStruct((KV_HEAD...]
    pallas_call x2, Pallas kernels: 73 us -> 56.9 us  [feature_slices(): pl.pallas_call(slices_kernel, out_shape=jax.ShapeDtypeStruct((levels, pla...]
    dot_general x8 -> x0, matrix products: 5.89 us -> none  [the longest x4 3.12 us: attend(): jnp.einsum('qhgd,khd->hgqk', query_all, block_keys, preferred_element_typ...]
    pallas_call x6, Pallas kernels: 177 us -> 172 us  [exchange(): pl.pallas_call(functools.partial(exchange_kernel, along, mode), out_shape...]
  transfers between devices with their start and end apart: 8 -> 8, of which waited for: 0 -> 0; matrix products, arithmetic and copies ran while one was open for 13% -> 9% of each run, Pallas kernels for 33% -> 34%
where the time goes in v3:
time: 313 us; the launch traced here: 312 us
  Pallas kernels  248 us (79%)
  other arithmetic  23.9 us (8%)
  local copies, waits for them, and re-layouts  17.6 us (6%)
  matrix products  16.2 us (5%)
  starting transfers between devices  4.09 us (1%)
    pallas_call x6, Pallas kernels, exchange(): pl.pallas_call(functools.partial(exchange_kernel, along, mode), out_shape...  172 us
    pallas_call x2, Pallas kernels, feature_slices(): pl.pallas_call(slices_kernel, out_shape=jax.ShapeDtypeStruct((levels, pla...  56.9 us
    pallas_call x1, Pallas kernels, attend(): pl.pallas_call(attention_kernel, out_shape=[jax.ShapeDtypeStruct((KV_HEAD...  19 us
  transfers between devices with their start and end apart: 8, of which 0 were waited for; matrix products, arithmetic and copies ran while one was open for 9% of the time, Pallas kernels for 34%

profile of v3, /device:TPU:0, one launch (start us, length us, event | category | flops | bytes accessed | tf_op | source)
XLA Modules:
  0.0 312.1 jit_solution(8639545930112731262)
XLA Ops:
  0.7 3.2 %constant_dynamic-slice_fusion.3 = (bf16[512,768]{1,0:T(8,128)(2,1)}, bf16[512,768]{1,0:T(8,128)(2,1)S(1)}, bf16[512,768]{1,0:T(8,128)(2,1)S(1)}, bf16[512,768]{1,0:T(8,128)(2,1)}) fusion(bf16[512,1536]{1,0:T(8,128)(2,1)} %param.30, s32[]{:T(128)S(6)} %select_n.96, s32[]{:T(128)S(6)} %select_n.97, bf16[512,1536]{1,0:T(8,128)(2,1)} %param.29), kind=kLoop, calls=%fused_computation.112 | loop fusion | bytes 6291464 | tf_op jit(solution)/shard_map/dynamic_slice | solution.py:220
  3.9 1.3 pad_maximum_fusion.1
  5.2 2.9 collective-permute-start.5
  17.5 2.1 constant_dynamic-slice_fusion
  20.5 1.6 copy-done.2
  22.1 19.0 %shard_map.167 = (f32[8,256,1]{2,1,0:T(8,128)S(1)}, f32[8,256,1]{2,1,0:T(8,128)S(1)}, f32[8,256,128]{2,1,0:T(8,128)S(1)}) custom-call(s32[1]{0:T(128)} %bitcast.1.limit_ref, bf16[64,4096]{1,0:T(8,128)(2,1)S(1)} %pad_maximum_fusion.2.query_ref, bf16[1024,1024]{1,0:T(8,128)(2,1)S(1)} %copy-done.1, bf16[1024,1024]{1,0:T(8,128)(2,1)S(1)} %copy-done.2, ...), custom_call_target="tpu_custom_call" | custom-call | flops 1073741824 | bytes 4194304 | tf_op jit(solution)/shard_map/pallas_call | solution.py:293
  41.1 1.0 copy-done.3
  42.1 1.0 copy-done.4
  44.0 1.6 reduce.2
  46.7 1.8 convolution_convert_fusion.1
  49.2 2.1 fusion.22
  52.1 32.5 %shard_map.168 = bf16[4,8,32,1024]{3,2,1,0:T(8,128)(2,1)} custom-call(bf16[32,4096]{1,0:T(8,128)(2,1)} %convert_element_type.136.rows_ref), custom_call_target="tpu_custom_call" | custom-call | tf_op jit(solution)/shard_map/pallas_call | solution.py:198
  84.7 1.4 broadcast_select_fusion.5
  86.4 2.2 convolution_convert_fusion.3
  88.6 22.3 %shard_map.169 = bf16[4,256,512]{2,1,0:T(8,128)(2,1)} custom-call(bf16[4,256,512]{2,1,0:T(8,128)(2,1)} %bitcast.94), custom_call_target="tpu_custom_call" | custom-call | tf_op jit(solution)/shard_map/pallas_call | solution.py:113
  111.0 2.2 reduce_sum.72
  113.1 6.6 %shard_map.170 = bf16[8,32,512]{2,1,0:T(8,128)(2,1)} custom-call(bf16[8,32,512]{2,1,0:T(8,128)(2,1)} %bitcast.92), custom_call_target="tpu_custom_call" | custom-call | tf_op jit(solution)/shard_map/pallas_call | solution.py:113
  119.7 1.2 copy.68
  121.4 1.3 fusion.12
  123.5 24.4 %shard_map.171 = bf16[4,8,32,1024]{3,2,1,0:T(8,128)(2,1)} custom-call(bf16[32,4096]{1,0:T(8,128)(2,1)} %fusion.14.rows_ref), custom_call_target="tpu_custom_call" | custom-call | tf_op jit(solution)/shard_map/pallas_call | solution.py:198
  147.9 1.2 broadcast_select_fusion.3
  149.6 2.2 broadcast_select_fusion.1
  151.7 4.9 %convolution_convert_fusion = bf16[1024,1536]{1,0:T(8,128)(2,1)} fusion(bf16[1024,1024]{1,0:T(8,128)(2,1)S(1)} %bitcast.84, bf16[512,1536]{1,0:T(8,128)(2,1)S(1)} %get-tuple-element.11, bf16[512,1536]{1,0:T(8,128)(2,1)S(1)} %get-tuple-element.10), kind=kOutput, calls=%fused_computation.1 | convolution fusion | flops 3229089792 | bytes 8388608 | tf_op jit(solution)/shard_map/dot_general | solution.py:452
  156.6 55.4 %shard_map.172 = bf16[4,256,1536]{2,1,0:T(8,128)(2,1)} custom-call(bf16[4,256,1536]{2,1,0:T(8,128)(2,1)} %bitcast.83), custom_call_target="tpu_custom_call" | custom-call | tf_op jit(solution)/shard_map/pallas_call | solution.py:113
  212.0 2.6 convert_reduce_fusion
  214.6 1.0 fusion.11.rows_ref
  215.6 45.2 %shard_map.173 = bf16[4,256,768]{2,1,0:T(8,128)(2,1)} custom-call(bf16[256,768]{1,0:T(8,128)(2,1)} %fusion.11.rows_ref), custom_call_target="tpu_custom_call" | custom-call | tf_op jit(solution)/shard_map/pallas_call | solution.py:113
  260.8 4.5 %convolution_convert_fusion.2 = bf16[1024,1024]{1,0:T(8,128)(2,1)} fusion(bf16[1024,768]{1,0:T(8,128)(2,1)} %bitcast.89, bf16[768,512]{1,0:T(8,128)(2,1)S(1)} %copy-done.14, bf16[768,512]{1,0:T(8,128)(2,1)S(1)} %get-tuple-element.12), kind=kOutput, calls=%fused_computation.6 | convolution fusion | flops 1614807040 | bytes 5242880 | tf_op jit(solution)/shard_map/dot_general | solution.py:458
  265.3 25.5 %shard_map.174 = bf16[8,4,32,1024]{3,2,1,0:T(8,128)(2,1)} custom-call(bf16[4,8,32,1024]{3,2,1,0:T(8,128)(2,1)} %bitcast.86), custom_call_target="tpu_custom_call" | custom-call | tf_op jit(solution)/shard_map/pallas_call | solution.py:113
  290.8 2.7 reduce_sum.75.rows_ref
  293.6 16.7 %shard_map.175 = bf16[4,32,1024]{2,1,0:T(8,128)(2,1)} custom-call(bf16[4,32,1024]{2,1,0:T(8,128)(2,1)} %reduce_sum.75.rows_ref), custom_call_target="tpu_custom_call" | custom-call | tf_op jit(solution)/shard_map/pallas_call | solution.py:113
  310.3 1.0 convert_bitcast_fusion
  (119 shorter events, 15.0 us)
Async XLA Ops:
  0.6 7.5 %copy-start = (s32[16,64]{1,0:T(8,128)S(1)}, s32[16,64]{1,0:T(8,128)}, u32[]{:S(2)}) copy-start(s32[16,64]{1,0:T(8,128)} %param.23) | copy-start | bytes 12292
  3.9 5.8 %copy-start.18 = (s32[16]{0:T(128)S(1)}, s32[16]{0:T(128)}, u32[]{:S(2)}) copy-start(s32[16]{0:T(128)} %param.22) | copy-start | bytes 196
  3.9 7.0 %copy-start.15 = (bf16[32,4096]{1,0:T(8,128)(2,1)S(1)}, bf16[32,4096]{1,0:T(8,128)(2,1)}, u32[]{:S(2)}) copy-start(bf16[32,4096]{1,0:T(8,128)(2,1)} %param.17) | copy-start | bytes 786436
  5.2 6.2 %copy-start.19 = (bf16[128]{0:T(256)(128)(2,1)S(1)}, bf16[128]{0:T(256)(128)(2,1)}, u32[]{:S(2)}) copy-start(bf16[128]{0:T(256)(128)(2,1)} %param.25) | copy-start | bytes 772
  5.2 143.9 %collective-permute-start.5 = (bf16[512,1536]{1,0:T(8,128)(2,1)}, bf16[512,1536]{1,0:T(8,128)(2,1)}, u32[]{:S(2)}, u32[]{:S(2)}) collective-permute-start(bf16[512,1536]{1,0:T(8,128)(2,1)} %pad_maximum_fusion.1), channel_id=1, source_target_pairs={{0,4},{4,0},{8,12},{12,8},{16,20},{20,16},{24,28},{28,24},{1,5},{5... | collective-permute-start | bytes 4718600 | tf_op jit(solution)/shard_map/ppermute | solution.py:23
  11.3 1.2 copy-start.12
  11.9 1.6 copy-start.16
  11.9 1.7 copy-start.20
  12.1 2.5 copy-start.6
  12.1 3.7 %copy-start.21 = (s32[16]{0:T(128)S(1)}, s32[16]{0:T(128)}, u32[]{:S(2)}) copy-start(s32[16]{0:T(128)} %param.24) | copy-start | bytes 196
  12.4 8.0 %collective-permute-start = (bf16[32,4096]{1,0:T(8,128)(2,1)S(1)}, bf16[32,4096]{1,0:T(8,128)(2,1)S(1)}, u32[]{:S(2)}, u32[]{:S(2)}) collective-permute-start(bf16[32,4096]{1,0:T(8,128)(2,1)S(1)} %bitcast.95), channel_id=1, source_target_pairs={{0,1},{1,0},{2,3},{3,2},{4,5},{5,4},{6,7},{7,6},{8,9},{9,8},{10,11... | collective-permute-start | bytes 786440 | tf_op jit(solution)/shard_map/ppermute | solution.py:23
  13.4 6.8 %copy-start.17 = (bf16[4096]{0:T(1024)(128)(2,1)S(1)}, bf16[4096]{0:T(1024)(128)(2,1)}, u32[]{:S(2)}) copy-start(bf16[4096]{0:T(1024)(128)(2,1)} %param.27) | copy-start | bytes 24580
  13.4 71.3 %collective-permute-start.4 = (bf16[512,512]{1,0:T(8,128)(2,1)}, bf16[512,512]{1,0:T(8,128)(2,1)}, u32[]{:S(2)}, u32[]{:S(2)}) collective-permute-start(bf16[512,512]{1,0:T(8,128)(2,1)} %constant_dynamic-slice_fusion.5), channel_id=1, source_target_pairs={{0,4},{4,0},{8,12},{12,8},{16,20},{20,16},{24,28},{28,24},{1,5},{5... | collective-permute-start | bytes 1572872 | tf_op jit(solution)/shard_map/ppermute | solution.py:23
  13.6 6.9 %copy-start.1 = (bf16[1024,1024]{1,0:T(8,128)(2,1)S(1)}, bf16[1024,1024]{1,0:T(8,128)(2,1)}, u32[]{:S(2)}) copy-start(bf16[1024,1024]{1,0:T(8,128)(2,1)} %key_ref.1) | copy-start | bytes 6291460
  15.2 31.5 %collective-permute-start.7 = (bf16[32,2048]{1,0:T(8,128)(2,1)}, bf16[32,2048]{1,0:T(8,128)(2,1)}, u32[]{:S(2)}, u32[]{:S(2)}) collective-permute-start(bf16[32,2048]{1,0:T(8,128)(2,1)} %constant_dynamic-update-slice_fusion), channel_id=1, source_target_pairs={{0,1},{1,0},{2,3},{3,2},{4,5},{5,4},{6,7},{7,6},{8,9},{9,8},{10,11... | collective-permute-start | bytes 393224 | tf_op jit(solution)/shard_map/ppermute | solution.py:23
  20.5 1.6 copy-start.2
  41.1 1.0 copy-start.3
  42.1 1.0 copy-start.4
  43.1 5.4 %copy-start.5 = (f32[8,256,128]{2,1,0:T(8,128)S(1)}, f32[8,256,128]{2,1,0:T(8,128)}, u32[]{:S(2)}) copy-start(f32[8,256,128]{2,1,0:T(8,128)} %copy-done.4) | copy-start | bytes 3145732
  44.0 5.2 %collective-permute-start.2 = (bf16[8,4,32,128]{3,1,0,2:T(4,128)(2,1)}, bf16[8,4,32,128]{3,1,0,2:T(4,128)(2,1)}, u32[]{:S(2)}, u32[]{:S(2)}) collective-permute-start(bf16[8,4,32,128]{3,1,0,2:T(4,128)(2,1)} %copy.67), channel_id=1, source_target_pairs={{0,1},{1,0},{2,3},{3,2},{4,5},{5,4},{6,7},{7,6},{8,9},{9,8},{10,11... | collective-permute-start | bytes 786440 | tf_op jit(solution)/shard_map/ppermute | solution.py:23
  45.7 2.9 collective-permute-start.1
  46.7 2.0 collective-permute-start.3
  48.6 99.3 %collective-permute-start.6 = (bf16[768,512]{1,0:T(8,128)(2,1)}, bf16[768,512]{1,0:T(8,128)(2,1)S(1)}, u32[]{:S(2)}, u32[]{:S(2)}) collective-permute-start(bf16[768,512]{1,0:T(8,128)(2,1)} %constant_dynamic-slice_fusion), channel_id=1, source_target_pairs={{0,4},{4,0},{8,12},{12,8},{16,20},{20,16},{24,28},{28,24},{1,5},{5... | collective-permute-start | bytes 2359304 | tf_op jit(solution)/shard_map/ppermute | solution.py:23
  49.2 35.5 %copy-start.13 = (bf16[512,1024]{1,0:T(8,128)(2,1)S(1)}, bf16[512,1024]{1,0:T(8,128)(2,1)}, u32[]{:S(2)}) copy-start(bf16[512,1024]{1,0:T(8,128)(2,1)} %param.28) | copy-start | bytes 3145732
  84.7 1.7 copy-start.10
  121.4 26.6 %copy-start.11 = (bf16[1536,512]{1,0:T(8,128)(2,1)S(1)}, bf16[1536,512]{1,0:T(8,128)(2,1)}, u32[]{:S(2)}) copy-start(bf16[1536,512]{1,0:T(8,128)(2,1)} %param.31) | copy-start | bytes 4718596
  147.9 1.2 copy-start.7
  147.9 1.6 copy-start.8
  149.6 2.2 copy-start.9
  214.6 46.2 %copy-start.14 = (bf16[768,512]{1,0:T(8,128)(2,1)S(1)}, bf16[768,512]{1,0:T(8,128)(2,1)}, u32[]{:S(2)}) copy-start(bf16[768,512]{1,0:T(8,128)(2,1)} %get-tuple-element.13) | copy-start | bytes 2359300

commit v4 on v3

--- a/solution.py
+++ b/solution.py
@@ -66,25 +66,27 @@
     )
 
 
-def exchange_kernel(along, mode, rows_ref, out_ref, send_sem, recv_sem, own_sem):
+def line_of(along):
     tp_count = lax.axis_size("tp")
     req, tp = lax.axis_index("req"), lax.axis_index("tp")
     level, side = req // SIDE, req % SIDE
     if along == "level":
-        count, mine = lax.axis_size("req") // SIDE, level
-    else:
-        count, mine = SIDE * tp_count, side * tp_count + tp
-
-    def device(index):
-        if along == "level":
-            return {"req": index * SIDE + side, "tp": tp}
-        return {"req": level * SIDE + index // tp_count, "tp": index % tp_count}
+        return (
+            lax.axis_size("req") // SIDE,
+            level,
+            lambda index: {"req": index * SIDE + side, "tp": tp},
+        )
+    return (
+        SIDE * tp_count,
+        side * tp_count + tp,
+        lambda index: {"req": level * SIDE + index // tp_count, "tp": index % tp_count},
+    )
+
+
+def exchange_kernel(along, rows_ref, out_ref, send_sem, recv_sem, own_sem):
+    count, mine, device = line_of(along)
 
     def part(index):
-        if mode == "copy":
-            return rows_ref
-        if mode == "inner":
-            return rows_ref.at[:, index]
         return rows_ref.at[index]
 
     others = [(mine + step) % count for step in range(1, count)]
@@ -102,22 +104,175 @@
     own.wait()
 
 
-def exchange(rows, along, mode, collective_id):
+def exchange(rows, along, collective_id):
     count = lax.axis_size("req") // SIDE if along == "level" else SIDE * lax.axis_size("tp")
-    if mode == "copy":
-        part_shape = rows.shape
-    elif mode == "inner":
-        part_shape = rows.shape[:1] + rows.shape[2:]
-    else:
-        part_shape = rows.shape[1:]
+    part_shape = rows.shape[1:]
     return pl.pallas_call(
-        functools.partial(exchange_kernel, along, mode),
+        functools.partial(exchange_kernel, along),
         out_shape=jax.ShapeDtypeStruct((count, *part_shape), rows.dtype),
         in_specs=[ANY],
         out_specs=ANY,
         scratch_shapes=[
             pltpu.SemaphoreType.DMA((count - 1,)),
             pltpu.SemaphoreType.DMA((count - 1,)),
+            pltpu.SemaphoreType.DMA,
+        ],
+        compiler_params=pltpu.CompilerParams(collective_id=collective_id, has_side_effects=True),
+    )(rows)
+
+
+def reduce_kernel(
+    along, mode, rows_ref, out_ref, landed, held,
+    pair_send, pair_recv, far_send, far_recv, last_send, last_recv, own_sems,
+):
+    count, mine, device = line_of(along)
+    half, place, parity = count // 2, mine // 2, mine % 2
+    depth = landed.shape[1]
+    piece = depth // 2
+
+    def part(index, start, size):
+        if mode == "inner":
+            return rows_ref.at[pl.ds(start, size), index]
+        return rows_ref.at[index, pl.ds(start, size)]
+
+    order = [(place + step) % half for step in range(1, half)]
+    pair = device(place * 2 + 1 - parity)
+    far_devices = [device(index * 2 + parity) for index in order]
+    meet(far_devices + [pair])
+    inward, kept, outward = [], [], []
+    for at, index in enumerate(order):
+        for cut in range(2):
+            copy = remote(
+                part(index * 2 + 1 - parity, cut * piece, piece),
+                landed.at[at, pl.ds(cut * piece, piece)],
+                pair_send.at[at * 2 + cut],
+                pair_recv.at[at * 2 + cut],
+                pair,
+            )
+            copy.start()
+            inward.append(copy)
+        copy = pltpu.make_async_copy(
+            part(index * 2 + parity, 0, depth), held.at[at], own_sems.at[at + 1]
+        )
+        copy.start()
+        kept.append(copy)
+    last = remote(
+        part(place * 2 + 1 - parity, 0, depth), out_ref.at[1], last_send, last_recv, pair
+    )
+    last.start()
+    own = pltpu.make_async_copy(part(mine, 0, depth), out_ref.at[0], own_sems.at[0])
+    own.start()
+    for at, peer in enumerate(far_devices):
+        kept[at].wait()
+        for cut in range(2):
+            inward[at * 2 + cut].wait_recv()
+
+            @pl.loop(cut * piece, (cut + 1) * piece)
+            def _(row):
+                total = held[at, row].astype(jnp.float32) + landed[at, row].astype(jnp.float32)
+                held[at, row] = total.astype(held.dtype)
+
+            copy = remote(
+                held.at[at, pl.ds(cut * piece, piece)],
+                out_ref.at[at + 2, pl.ds(cut * piece, piece)],
+                far_send.at[at * 2 + cut],
+                far_recv.at[at * 2 + cut],
+                peer,
+            )
+            copy.start()
+            outward.append(copy)
+    own.wait()
+    last.wait()
+    for copy in inward:
+        copy.wait_send()
+    for copy in outward:
+        copy.wait()
+
+
+def reduced(rows, along, mode, collective_id):
+    count = lax.axis_size("req") // SIDE if along == "level" else SIDE * lax.axis_size("tp")
+    half = count // 2
+    if mode == "inner":
+        part_shape = rows.shape[:1] + rows.shape[2:]
+    else:
+        part_shape = rows.shape[1:]
+    parts = pl.pallas_call(
+        functools.partial(reduce_kernel, along, mode),
+        out_shape=jax.ShapeDtypeStruct((half + 1, *part_shape), rows.dtype),
+        in_specs=[ANY],
+        out_specs=ANY,
+        scratch_shapes=[
+            pltpu.VMEM((half - 1, *part_shape), rows.dtype),
+            pltpu.VMEM((half - 1, *part_shape), rows.dtype),
+            pltpu.SemaphoreType.DMA((2 * (half - 1),)),
+            pltpu.SemaphoreType.DMA((2 * (half - 1),)),
+            pltpu.SemaphoreType.DMA((2 * (half - 1),)),
+            pltpu.SemaphoreType.DMA((2 * (half - 1),)),
+            pltpu.SemaphoreType.DMA,
+            pltpu.SemaphoreType.DMA,
+            pltpu.SemaphoreType.DMA((half,)),
+        ],
+        compiler_params=pltpu.CompilerParams(
+            collective_id=collective_id, has_side_effects=True, vmem_limit_bytes=40 * 2**20
+        ),
+    )(rows)
+    return jnp.sum(parts.astype(jnp.float32), axis=0)
+
+
+def gather_kernel(rows_ref, out_ref, far_send, far_recv, near_send, near_recv, own_sem):
+    count, mine, device = line_of("level")
+    half, place, parity = count // 2, mine // 2, mine % 2
+    pair = device(place * 2 + 1 - parity)
+    order = [(place + step) % half for step in range(1, half)]
+    far_devices = [device(index * 2 + parity) for index in order]
+    meet(far_devices + [pair])
+    far, near = [], []
+    for cut in range(2):
+        for peer in far_devices:
+            at = len(far)
+            copy = remote(
+                rows_ref.at[cut], out_ref.at[mine, cut], far_send.at[at], far_recv.at[at], peer
+            )
+            copy.start()
+            far.append(copy)
+    own = pltpu.make_async_copy(rows_ref, out_ref.at[mine], own_sem)
+    own.start()
+    for cut in range(2):
+        at = len(near)
+        copy = remote(
+            rows_ref.at[cut], out_ref.at[mine, cut], near_send.at[at], near_recv.at[at], pair
+        )
+        copy.start()
+        near.append(copy)
+    for cut in range(2):
+        for step in range(1, half):
+            far[cut * (half - 1) + step - 1].wait_recv()
+            landed = out_ref.at[((place - step + half) % half) * 2 + parity, cut]
+            at = len(near)
+            copy = remote(landed, landed, near_send.at[at], near_recv.at[at], pair)
+            copy.start()
+            near.append(copy)
+    own.wait()
+    for copy in near:
+        copy.wait()
+    for copy in far:
+        copy.wait_send()
+
+
+def gathered_levels(rows, collective_id):
+    count = lax.axis_size("req") // SIDE
+    half = count // 2
+    rows = rows.reshape(2, rows.shape[0] // 2, rows.shape[1])
+    return pl.pallas_call(
+        gather_kernel,
+        out_shape=jax.ShapeDtypeStruct((count, *rows.shape), rows.dtype),
+        in_specs=[ANY],
+        out_specs=ANY,
+        scratch_shapes=[
+            pltpu.SemaphoreType.DMA((2 * (half - 1),)),
+            pltpu.SemaphoreType.DMA((2 * (half - 1),)),
+            pltpu.SemaphoreType.DMA((2 * half,)),
+            pltpu.SemaphoreType.DMA((2 * half,)),
             pltpu.SemaphoreType.DMA,
         ],
         compiler_params=pltpu.CompilerParams(collective_id=collective_id, has_side_effects=True),
@@ -360,10 +515,8 @@
     gate_up_received = swapped(jnp.concatenate([gate_sent, up_sent], axis=1), "req", 0)
     gate_up_kept = jnp.concatenate([gate_kept, up_kept], axis=1)
     down_kept, down_sent = paired_halves(down_weight, 0)
-    down_received = swapped(down_sent, "req", 0)
     out_full = joined(out_kept, out_received, 0)
     gate_up_full = joined(gate_up_kept, gate_up_received, 0)
-    down_full = joined(down_kept, down_received, 1)
     tree_size = 2 * half_rows
     kv_width = new_keys.shape[1]
     q_width = queries.shape[1]
@@ -432,11 +585,12 @@
     levels = lax.axis_size("req") // SIDE
     places = SIDE * tp_count
     attn_slice = feature_slices(attended, 0)
+    attn_slice, down_sent = lax.optimization_barrier((attn_slice, down_sent))
+    down_full = joined(down_kept, swapped(down_sent, "req", 0), 1)
     projected = jnp.dot(attn_slice, out_full, preferred_element_type=jnp.float32)
-    projected = projected.astype(jnp.bfloat16).reshape(levels, places * half_rows, -1)
-    projected = exchange(projected, "level", "lead", 1)
-    projected = jnp.sum(projected.astype(jnp.float32), axis=0).astype(jnp.bfloat16)
-    projected = exchange(projected.reshape(places, half_rows, -1), "place", "lead", 2)
+    projected = projected.astype(jnp.bfloat16).reshape(levels, places, half_rows, -1)
+    projected = reduced(projected, "level", "lead", 1).astype(jnp.bfloat16)
+    projected = exchange(projected.reshape(places, half_rows, -1), "place", 2)
     own_projected = jnp.transpose(
         projected.reshape(SIDE, tp_count, half_rows, -1), (2, 1, 0, 3)
     ).reshape(half_rows, -1)
@@ -450,16 +604,15 @@
     )
     normed_slice = feature_slices(normed, 3)
     sums = jnp.dot(normed_slice, gate_up_full, preferred_element_type=jnp.float32)
-    sums = sums.astype(jnp.bfloat16).reshape(levels, places * half_rows, -1)
-    sums = jnp.sum(exchange(sums, "level", "lead", 4).astype(jnp.float32), axis=0)
+    sums = sums.astype(jnp.bfloat16).reshape(levels, places, half_rows, -1)
+    sums = reduced(sums, "level", "lead", 4).reshape(places * half_rows, -1)
     hidden_width = sums.shape[1] // 2
     hidden = (jax.nn.silu(sums[:, :hidden_width]) * sums[:, hidden_width:]).astype(jnp.bfloat16)
-    hidden_all = exchange(hidden, "level", "copy", 5).reshape(-1, hidden_width)
+    hidden_all = gathered_levels(hidden, 5).reshape(-1, hidden_width)
     partial_out = jnp.dot(hidden_all, down_full, preferred_element_type=jnp.float32)
     partial_out = partial_out.astype(jnp.bfloat16).reshape(levels, places, half_rows, -1)
-    paired_sum = exchange(partial_out, "place", "inner", 6).astype(jnp.float32)
-    paired_sum = jnp.sum(paired_sum, axis=0).astype(jnp.bfloat16)
-    mlp_own = exchange(paired_sum, "level", "lead", 7)
+    paired_sum = reduced(partial_out, "place", "inner", 6).astype(jnp.bfloat16)
+    mlp_own = exchange(paired_sum, "level", 7)
     mlp_own = jnp.transpose(mlp_own, (1, 0, 2)).reshape(half_rows, -1).astype(jnp.float32)
     layer_out = (residual_wide + mlp_own).astype(jnp.bfloat16)
     return (layer_out, accepted_kv)

time: 313 us -> 264 us (0.84)
  Pallas kernels: 248 us -> 206 us
  matrix products: 16.2 us -> 12.6 us
  other arithmetic: 23.9 us -> 20.6 us
    pallas_call x6, Pallas kernels: 172 us -> 135 us  [the longest x3 90.9 us: reduced(): pl.pallas_call(functools.partial(reduce_kernel, along, mode), out_shape=j...]
    pallas_call x1, Pallas kernels: 19 us -> 8.32 us  [attend(): pl.pallas_call(attention_kernel, out_shape=[jax.ShapeDtypeStruct((KV_HEAD...]
    pallas_call x2, Pallas kernels: 56.9 us -> 63.1 us  [feature_slices(): pl.pallas_call(slices_kernel, out_shape=jax.ShapeDtypeStruct((levels, pla...]
    reduce_sum x3, other arithmetic: 7.44 us -> 2.27 us  [reduced(): return jnp.sum(parts.astype(jnp.float32), axis=0)]
    unnamed x50 -> x54, local copies, waits for them, and re-layouts: 6.15 us -> 6.35 us
  transfers between devices with their start and end apart: 8 -> 8, of which waited for: 0 -> 0; matrix products, arithmetic and copies ran while one was open for 9% -> 10% of each run, Pallas kernels for 34% -> 37%
where the time goes in v4:
time: 264 us; the launch traced here: 263 us
  Pallas kernels  206 us (78%)
  other arithmetic  20.6 us (8%)
  local copies, waits for them, and re-layouts  16.4 us (6%)
  matrix products  12.6 us (5%)
  starting transfers between devices  4.63 us (2%)
  between operations  2.69 us (1%)
    pallas_call x3, Pallas kernels, reduced(): pl.pallas_call(functools.partial(reduce_kernel, along, mode), out_shape=j...  90.9 us
    pallas_call x2, Pallas kernels, feature_slices(): pl.pallas_call(slices_kernel, out_shape=jax.ShapeDtypeStruct((levels, pla...  63.1 us
    pallas_call x1, Pallas kernels, gathered_levels(): pl.pallas_call(gather_kernel, out_shape=jax.ShapeDtypeStruct((count, *row...  27.9 us
    pallas_call x2, Pallas kernels, exchange(): pl.pallas_call(functools.partial(exchange_kernel, along), out_shape=jax.S...  16.1 us
    pallas_call x1, Pallas kernels, attend(): pl.pallas_call(attention_kernel, out_shape=[jax.ShapeDtypeStruct((KV_HEAD...  8.32 us
    unnamed x54, local copies, waits for them, and re-layouts  6.35 us
  transfers between devices with their start and end apart: 8, of which 0 were waited for; matrix products, arithmetic and copies ran while one was open for 10% of the time, Pallas kernels for 37%

profile of v4, /device:TPU:0, one launch (start us, length us, event | category | flops | bytes accessed | tf_op | source)
XLA Modules:
  0.0 263.3 jit_solution(4939486116166247038)
XLA Ops:
  2.9 1.2 dynamic_slice.35
  4.8 1.0 convert_bitcast_fusion.1
  7.7 1.9 constant_dynamic-slice_fusion.4
  9.6 2.8 %collective-permute-start.4 = (bf16[512,512]{1,0:T(8,128)(2,1)}, bf16[512,512]{1,0:T(8,128)(2,1)}, u32[]{:S(2)}, u32[]{:S(2)}) collective-permute-start(bf16[512,512]{1,0:T(8,128)(2,1)} %constant_dynamic-slice_fusion.4), channel_id=1, source_target_pairs={{0,4},{4,0},{8,12},{12,8},{16,20},{20,16},{24,28},{28,24},{1,5},{5... | collective-permute-start | bytes 1572872 | tf_op jit(solution)/shard_map/ppermute | solution.py:23
  12.4 1.4 constant_dynamic-slice_fusion.2
  13.8 1.3 pad_maximum_fusion.1
  21.1 1.0 pad_maximum_fusion.2.query_ref
  22.1 1.6 copy-done.2
  23.7 8.3 %shard_map.167 = (f32[8,256,1]{2,1,0:T(8,128)S(1)}, f32[8,256,1]{2,1,0:T(8,128)S(1)}, f32[8,256,128]{2,1,0:T(8,128)S(1)}) custom-call(s32[1]{0:T(128)} %bitcast.1.limit_ref, bf16[64,4096]{1,0:T(8,128)(2,1)S(1)} %pad_maximum_fusion.2.query_ref, bf16[1024,1024]{1,0:T(8,128)(2,1)S(1)} %copy-done.1, bf16[1024,1024]{1,0:T(8,128)(2,1)S(1)} %copy-done.2, ...), custom_call_target="tpu_custom_call" | custom-call | flops 1073741824 | bytes 4194304 | tf_op jit(solution)/shard_map/pallas_call | solution.py:448
  32.1 1.0 copy-done.3
  33.1 1.0 copy-done.4
  34.9 1.6 reduce.2
  37.7 1.8 convolution_convert_fusion.1
  40.1 2.1 fusion.22
  43.0 31.7 %shard_map.168 = bf16[4,8,32,1024]{3,2,1,0:T(8,128)(2,1)} custom-call(bf16[32,4096]{1,0:T(8,128)(2,1)} %convert_element_type.136.rows_ref), custom_call_target="tpu_custom_call" | custom-call | tf_op jit(solution)/shard_map/pallas_call | solution.py:353
  74.8 1.4 broadcast_select_fusion.5
  76.5 1.2 convolution_convert_fusion.3
  77.8 20.0 %shard_map.169 = bf16[3,8,32,512]{3,2,1,0:T(8,128)(2,1)S(1)} custom-call(bf16[4,8,32,512]{3,2,1,0:T(8,128)(2,1)S(1)} %bitcast.82), custom_call_target="tpu_custom_call" | custom-call | tf_op jit(solution)/shard_map/pallas_call | solution.py:199
  98.7 6.6 %shard_map.170 = bf16[8,32,512]{2,1,0:T(8,128)(2,1)} custom-call(bf16[8,32,512]{2,1,0:T(8,128)(2,1)} %reduce_sum.72.rows_ref), custom_call_target="tpu_custom_call" | custom-call | tf_op jit(solution)/shard_map/pallas_call | solution.py:110
  105.3 1.2 copy.68
  108.7 31.4 %shard_map.171 = bf16[4,8,32,1024]{3,2,1,0:T(8,128)(2,1)} custom-call(bf16[32,4096]{1,0:T(8,128)(2,1)} %fusion.14.rows_ref), custom_call_target="tpu_custom_call" | custom-call | tf_op jit(solution)/shard_map/pallas_call | solution.py:353
  140.2 1.5 broadcast_select_fusion.3
  141.8 2.2 broadcast_select_fusion.1
  143.9 3.6 %convolution_convert_fusion = bf16[1024,1536]{1,0:T(8,128)(2,1)S(1)} fusion(bf16[1024,1024]{1,0:T(8,128)(2,1)S(1)} %bitcast.88, bf16[512,1536]{1,0:T(8,128)(2,1)S(1)} %get-tuple-element.15, bf16[512,1536]{1,0:T(8,128)(2,1)S(1)} %get-tuple-element.14), kind=kOutput, calls=%fused_computation.1 | convolution fusion | flops 3229089792 | bytes 8388608 | tf_op jit(solution)/shard_map/dot_general | solution.py:606
  147.6 54.6 %shard_map.172 = bf16[3,8,32,1536]{3,2,1,0:T(8,128)(2,1)S(1)} custom-call(bf16[4,8,32,1536]{3,2,1,0:T(8,128)(2,1)S(1)} %bitcast.80), custom_call_target="tpu_custom_call" | custom-call | tf_op jit(solution)/shard_map/pallas_call | solution.py:199
  202.6 1.0 fusion.11
  203.6 27.9 %shard_map.173 = bf16[4,2,128,768]{3,2,1,0:T(8,128)(2,1)} custom-call(bf16[2,128,768]{2,1,0:T(8,128)(2,1)} %bitcast.93), custom_call_target="tpu_custom_call" | custom-call | tf_op jit(solution)/shard_map/pallas_call | solution.py:266
  231.5 3.2 %convolution_convert_fusion.2 = bf16[1024,1024]{1,0:T(8,128)(2,1)S(1)} fusion(bf16[1024,768]{1,0:T(8,128)(2,1)} %bitcast.92, bf16[768,512]{1,0:T(8,128)(2,1)S(1)} %get-tuple-element.17, bf16[768,512]{1,0:T(8,128)(2,1)S(1)} %get-tuple-element.16), kind=kOutput, calls=%fused_computation.6 | convolution fusion | flops 1614807040 | bytes 5242880 | tf_op jit(solution)/shard_map/dot_general | solution.py:612
  234.7 16.3 %shard_map.174 = bf16[5,4,32,1024]{3,2,1,0:T(8,128)(2,1)S(1)} custom-call(bf16[4,8,32,1024]{3,2,1,0:T(8,128)(2,1)S(1)} %bitcast.81), custom_call_target="tpu_custom_call" | custom-call | tf_op jit(solution)/shard_map/pallas_call | solution.py:199
  251.0 1.0 reduce_sum.75.rows_ref
  252.0 9.5 %shard_map.175 = bf16[4,32,1024]{2,1,0:T(8,128)(2,1)} custom-call(bf16[4,32,1024]{2,1,0:T(8,128)(2,1)} %reduce_sum.75.rows_ref), custom_call_target="tpu_custom_call" | custom-call | tf_op jit(solution)/shard_map/pallas_call | solution.py:110
  261.5 1.0 convert_bitcast_fusion
  (123 shorter events, 17.3 us)
Async XLA Ops:
  0.6 0.7 copy-start
  0.6 5.5 %copy-start.21 = (bf16[128]{0:T(256)(128)(2,1)S(1)}, bf16[128]{0:T(256)(128)(2,1)}, u32[]{:S(2)}) copy-start(bf16[128]{0:T(256)(128)(2,1)} %param.25) | copy-start | bytes 772
  6.6 5.8 %copy-start.13 = (bf16[512,1536]{1,0:T(8,128)(2,1)S(1)}, bf16[512,1536]{1,0:T(8,128)(2,1)}, u32[]{:S(2)}) copy-start(bf16[512,1536]{1,0:T(8,128)(2,1)} %param.30) | copy-start | bytes 4718596
  6.6 5.8 %copy-start.14 = (bf16[512,1536]{1,0:T(8,128)(2,1)S(1)}, bf16[512,1536]{1,0:T(8,128)(2,1)}, u32[]{:S(2)}) copy-start(bf16[512,1536]{1,0:T(8,128)(2,1)} %param.29) | copy-start | bytes 4718596
  7.2 13.9 %collective-permute-start = (bf16[32,4096]{1,0:T(8,128)(2,1)S(1)}, bf16[32,4096]{1,0:T(8,128)(2,1)}, u32[]{:S(2)}, u32[]{:S(2)}) collective-permute-start(bf16[32,4096]{1,0:T(8,128)(2,1)S(1)} %bitcast.97), channel_id=1, source_target_pairs={{0,1},{1,0},{2,3},{3,2},{4,5},{5,4},{6,7},{7,6},{8,9},{9,8},{10,11... | collective-permute-start | bytes 786440 | tf_op jit(solution)/shard_map/ppermute | solution.py:23
  9.6 65.2 %collective-permute-start.4 = (bf16[512,512]{1,0:T(8,128)(2,1)}, bf16[512,512]{1,0:T(8,128)(2,1)}, u32[]{:S(2)}, u32[]{:S(2)}) collective-permute-start(bf16[512,512]{1,0:T(8,128)(2,1)} %constant_dynamic-slice_fusion.4), channel_id=1, source_target_pairs={{0,4},{4,0},{8,12},{12,8},{16,20},{20,16},{24,28},{28,24},{1,5},{5... | collective-permute-start | bytes 1572872 | tf_op jit(solution)/shard_map/ppermute | solution.py:23
  13.8 1.3 copy-start.18
  13.8 1.5 copy-start.22
  13.8 2.5 copy-start.6
  13.8 3.3 %copy-start.23 = (s32[16]{0:T(128)S(1)}, s32[16]{0:T(128)}, u32[]{:S(2)}) copy-start(s32[16]{0:T(128)} %param.24) | copy-start | bytes 196
  13.8 4.9 %copy-start.11 = (bf16[1536,512]{1,0:T(8,128)(2,1)S(1)}, bf16[1536,512]{1,0:T(8,128)(2,1)}, u32[]{:S(2)}) copy-start(bf16[1536,512]{1,0:T(8,128)(2,1)} %param.31) | copy-start | bytes 4718596
  15.1 5.3 %copy-start.20 = (bf16[4096]{0:T(1024)(128)(2,1)S(1)}, bf16[4096]{0:T(1024)(128)(2,1)}, u32[]{:S(2)}) copy-start(bf16[4096]{0:T(1024)(128)(2,1)} %param.27) | copy-start | bytes 24580
  15.1 126.7 %collective-permute-start.5 = (bf16[512,1536]{1,0:T(8,128)(2,1)}, bf16[512,1536]{1,0:T(8,128)(2,1)}, u32[]{:S(2)}, u32[]{:S(2)}) collective-permute-start(bf16[512,1536]{1,0:T(8,128)(2,1)} %pad_maximum_fusion.1), channel_id=1, source_target_pairs={{0,4},{4,0},{8,12},{12,8},{16,20},{20,16},{24,28},{28,24},{1,5},{5... | collective-permute-start | bytes 4718600 | tf_op jit(solution)/shard_map/ppermute | solution.py:23
  15.3 6.8 %copy-start.1 = (bf16[1024,1024]{1,0:T(8,128)(2,1)S(1)}, bf16[1024,1024]{1,0:T(8,128)(2,1)}, u32[]{:S(2)}) copy-start(bf16[1024,1024]{1,0:T(8,128)(2,1)} %key_ref.1) | copy-start | bytes 6291460
  16.9 20.8 %collective-permute-start.7 = (bf16[32,2048]{1,0:T(8,128)(2,1)}, bf16[32,2048]{1,0:T(8,128)(2,1)}, u32[]{:S(2)}, u32[]{:S(2)}) collective-permute-start(bf16[32,2048]{1,0:T(8,128)(2,1)} %constant_dynamic-update-slice_fusion), channel_id=1, source_target_pairs={{0,1},{1,0},{2,3},{3,2},{4,5},{5,4},{6,7},{7,6},{8,9},{9,8},{10,11... | collective-permute-start | bytes 393224 | tf_op jit(solution)/shard_map/ppermute | solution.py:23
  22.1 1.6 copy-start.2
  32.0 1.0 copy-start.3
  33.1 1.0 copy-start.4
  34.1 5.4 %copy-start.5 = (f32[8,256,128]{2,1,0:T(8,128)S(1)}, f32[8,256,128]{2,1,0:T(8,128)}, u32[]{:S(2)}) copy-start(f32[8,256,128]{2,1,0:T(8,128)} %copy-done.4) | copy-start | bytes 3145732
  34.9 5.1 %collective-permute-start.2 = (bf16[8,4,32,128]{3,1,0,2:T(4,128)(2,1)}, bf16[8,4,32,128]{3,1,0,2:T(4,128)(2,1)}, u32[]{:S(2)}, u32[]{:S(2)}) collective-permute-start(bf16[8,4,32,128]{3,1,0,2:T(4,128)(2,1)} %copy.67), channel_id=1, source_target_pairs={{0,1},{1,0},{2,3},{3,2},{4,5},{5,4},{6,7},{7,6},{8,9},{9,8},{10,11... | collective-permute-start | bytes 786440 | tf_op jit(solution)/shard_map/ppermute | solution.py:23
  36.7 2.9 %collective-permute-start.1 = (bf16[8,4,32,1]{2,1,0,3:T(4,128)(2,1)S(1)}, bf16[8,4,32,1]{2,1,0,3:T(4,128)(2,1)S(1)}, u32[]{:S(2)}, u32[]{:S(2)}) collective-permute-start(bf16[8,4,32,1]{2,1,0,3:T(4,128)(2,1)S(1)} %slice.103), channel_id=1, source_target_pairs={{0,1},{1,0},{2,3},{3,2},{4,5},{5,4},{6,7},{7,6},{8,9},{9,8},{10,11... | collective-permute-start | bytes 6152 | tf_op jit(solution)/shard_map/ppermute | solution.py:23
  37.7 1.9 collective-permute-start.3
  40.0 34.7 %copy-start.15 = (bf16[512,1024]{1,0:T(8,128)(2,1)S(1)}, bf16[512,1024]{1,0:T(8,128)(2,1)}, u32[]{:S(2)}) copy-start(bf16[512,1024]{1,0:T(8,128)(2,1)} %param.28) | copy-start | bytes 3145732
  74.8 1.7 copy-start.10
  97.7 9.2 %copy-start.16 = (bf16[768,512]{1,0:T(8,128)(2,1)S(1)}, bf16[768,512]{1,0:T(8,128)(2,1)}, u32[]{:S(2)}) copy-start(bf16[768,512]{1,0:T(8,128)(2,1)} %constant_dynamic-slice_fusion.5) | copy-start | bytes 2359300
  97.8 9.9 %copy-start.17 = (bf16[32,4096]{1,0:T(8,128)(2,1)S(1)}, bf16[32,4096]{1,0:T(8,128)(2,1)}, u32[]{:S(2)}) copy-start(bf16[32,4096]{1,0:T(8,128)(2,1)} %param.16) | copy-start | bytes 786436
  97.8 10.1 %copy-start.19 = (f32[4096]{0:T(1024)S(1)}, f32[4096]{0:T(1024)}, u32[]{:S(2)}) copy-start(f32[4096]{0:T(1024)} %convert_element_type.144) | copy-start | bytes 49156
  107.0 33.2 %copy-start.12 = (bf16[1536,512]{1,0:T(8,128)(2,1)S(1)}, bf16[1536,512]{1,0:T(8,128)(2,1)}, u32[]{:S(2)}) copy-start(bf16[1536,512]{1,0:T(8,128)(2,1)} %param.31) | copy-start | bytes 4718596
  107.0 33.2 %collective-permute-start.6 = (bf16[768,512]{1,0:T(8,128)(2,1)S(1)}, bf16[768,512]{1,0:T(8,128)(2,1)}, u32[]{:S(2)}, u32[]{:S(2)}) collective-permute-start(bf16[768,512]{1,0:T(8,128)(2,1)S(1)} %copy-done.16), channel_id=1, source_target_pairs={{0,4},{4,0},{8,12},{12,8},{16,20},{20,16},{24,28},{28,24},{1,5},{5... | collective-permute-start | bytes 2359304 | tf_op jit(solution)/shard_map/ppermute | solution.py:23
  140.2 1.6 copy-start.7
  140.2 1.6 copy-start.8
  141.8 2.2 copy-start.9

commit v5 on v4

--- a/solution.py
+++ b/solution.py
@@ -585,8 +585,6 @@
     levels = lax.axis_size("req") // SIDE
     places = SIDE * tp_count
     attn_slice = feature_slices(attended, 0)
-    attn_slice, down_sent = lax.optimization_barrier((attn_slice, down_sent))
-    down_full = joined(down_kept, swapped(down_sent, "req", 0), 1)
     projected = jnp.dot(attn_slice, out_full, preferred_element_type=jnp.float32)
     projected = projected.astype(jnp.bfloat16).reshape(levels, places, half_rows, -1)
     projected = reduced(projected, "level", "lead", 1).astype(jnp.bfloat16)
@@ -603,6 +601,8 @@
         jnp.bfloat16
     )
     normed_slice = feature_slices(normed, 3)
+    normed_slice, down_sent = lax.optimization_barrier((normed_slice, down_sent))
+    down_full = joined(down_kept, swapped(down_sent, "req", 0), 1)
     sums = jnp.dot(normed_slice, gate_up_full, preferred_element_type=jnp.float32)
     sums = sums.astype(jnp.bfloat16).reshape(levels, places, half_rows, -1)
     sums = reduced(sums, "level", "lead", 4).reshape(places * half_rows, -1)

time: 264 us -> 267 us (1.011)
  waiting for transfers between devices: 0.02 us -> 16.7 us
  Pallas kernels: 206 us -> 193 us
    ppermute x8, waiting for transfers between devices: 0.02 us -> 16.7 us  [swapped(): return lax.ppermute(value, axis, pairs)]
    pallas_call x2, Pallas kernels: 63.1 us -> 46.8 us  [feature_slices(): pl.pallas_call(slices_kernel, out_shape=jax.ShapeDtypeStruct((levels, pla...]
    pallas_call x1, Pallas kernels: 8.32 us -> 11.9 us  [attend(): pl.pallas_call(attention_kernel, out_shape=[jax.ShapeDtypeStruct((KV_HEAD...]
    unnamed x54 -> x64, local copies, waits for them, and re-layouts: 6.35 us -> 6.4 us
  transfers between devices with their start and end apart: 8 -> 8, of which waited for: 0 -> 1; matrix products, arithmetic and copies ran while one was open for 10% -> 9% of each run, Pallas kernels for 37% -> 33%
where the time goes in v5:
time: 267 us; the launch traced here: 266 us
  Pallas kernels  193 us (72%)
  other arithmetic  18.8 us (7%)
  waiting for transfers between devices  16.7 us (6%)
  local copies, waits for them, and re-layouts  16.6 us (6%)
  matrix products  12.6 us (5%)
  starting transfers between devices  5.62 us (2%)
  between operations  2.7 us (1%)
    pallas_call x3, Pallas kernels, reduced(): pl.pallas_call(functools.partial(reduce_kernel, along, mode), out_shape=j...  91.1 us
    pallas_call x2, Pallas kernels, feature_slices(): pl.pallas_call(slices_kernel, out_shape=jax.ShapeDtypeStruct((levels, pla...  46.8 us
    pallas_call x1, Pallas kernels, gathered_levels(): pl.pallas_call(gather_kernel, out_shape=jax.ShapeDtypeStruct((count, *row...  27.8 us
    ppermute x8, waiting for transfers between devices, swapped(): return lax.ppermute(value, axis, pairs)  16.7 us
    pallas_call x2, Pallas kernels, exchange(): pl.pallas_call(functools.partial(exchange_kernel, along), out_shape=jax.S...  15.5 us
    pallas_call x1, Pallas kernels, attend(): pl.pallas_call(attention_kernel, out_shape=[jax.ShapeDtypeStruct((KV_HEAD...  11.9 us
    unnamed x64, local copies, waits for them, and re-layouts  6.4 us
    ppermute x8, starting transfers between devices, swapped(): return lax.ppermute(value, axis, pairs)  5.62 us
  transfers between devices with their start and end apart: 8, of which 1 were waited for; matrix products, arithmetic and copies ran while one was open for 9% of the time, Pallas kernels for 33%

profile of v5, /device:TPU:0, one launch (start us, length us, event | category | flops | bytes accessed | tf_op | source)
XLA Modules:
  0.0 266.1 jit_solution(15253216233498072249)
XLA Ops:
  2.9 1.2 dynamic_slice.35
  4.8 1.0 convert_bitcast_fusion.1
  7.7 1.9 constant_dynamic-slice_fusion.5
  9.6 2.8 %collective-permute-start.4 = (bf16[512,512]{1,0:T(8,128)(2,1)}, bf16[512,512]{1,0:T(8,128)(2,1)}, u32[]{:S(2)}, u32[]{:S(2)}) collective-permute-start(bf16[512,512]{1,0:T(8,128)(2,1)} %constant_dynamic-slice_fusion.5), channel_id=1, source_target_pairs={{0,4},{4,0},{8,12},{12,8},{16,20},{20,16},{24,28},{28,24},{1,5},{5... | collective-permute-start | bytes 1572872 | tf_op jit(solution)/shard_map/ppermute | solution.py:23
  12.5 1.4 constant_dynamic-slice_fusion.2
  13.8 1.3 pad_maximum_fusion.1
  19.6 1.0 pad_maximum_fusion.2.query_ref
  20.7 1.6 copy-done.2
  22.3 11.9 %shard_map.167 = (f32[8,256,1]{2,1,0:T(8,128)S(1)}, f32[8,256,1]{2,1,0:T(8,128)S(1)}, f32[8,256,128]{2,1,0:T(8,128)S(1)}) custom-call(s32[1]{0:T(128)} %bitcast.1.limit_ref, bf16[64,4096]{1,0:T(8,128)(2,1)S(1)} %pad_maximum_fusion.2.query_ref, bf16[1024,1024]{1,0:T(8,128)(2,1)S(1)} %copy-done.1, bf16[1024,1024]{1,0:T(8,128)(2,1)S(1)} %copy-done.2, ...), custom_call_target="tpu_custom_call" | custom-call | flops 1073741824 | bytes 4194304 | tf_op jit(solution)/shard_map/pallas_call | solution.py:448
  35.1 1.0 copy-done.4
  37.0 1.6 reduce.2
  41.7 2.1 fusion.22
  44.6 27.9 %shard_map.168 = bf16[4,8,32,1024]{3,2,1,0:T(8,128)(2,1)} custom-call(bf16[32,4096]{1,0:T(8,128)(2,1)} %convert_element_type.136.rows_ref), custom_call_target="tpu_custom_call" | custom-call | tf_op jit(solution)/shard_map/pallas_call | solution.py:353
  72.6 1.4 broadcast_select_fusion.5
  74.3 1.2 convolution_convert_fusion.3
  75.6 22.0 %shard_map.169 = bf16[3,8,32,512]{3,2,1,0:T(8,128)(2,1)S(1)} custom-call(bf16[4,8,32,512]{3,2,1,0:T(8,128)(2,1)S(1)} %bitcast.82), custom_call_target="tpu_custom_call" | custom-call | tf_op jit(solution)/shard_map/pallas_call | solution.py:199
  98.5 6.5 %shard_map.170 = bf16[8,32,512]{2,1,0:T(8,128)(2,1)} custom-call(bf16[8,32,512]{2,1,0:T(8,128)(2,1)} %reduce_sum.72.rows_ref), custom_call_target="tpu_custom_call" | custom-call | tf_op jit(solution)/shard_map/pallas_call | solution.py:110
  105.1 1.2 copy.68
  107.8 18.8 %shard_map.171 = bf16[4,8,32,1024]{3,2,1,0:T(8,128)(2,1)} custom-call(bf16[32,4096]{1,0:T(8,128)(2,1)} %fusion.14.rows_ref), custom_call_target="tpu_custom_call" | custom-call | tf_op jit(solution)/shard_map/pallas_call | solution.py:353
  126.7 1.2 collective-permute-start.6
  128.1 1.8 convolution_convert_fusion.1
  129.9 16.7 %collective-permute-done.6 = bf16[768,512]{1,0:T(8,128)(2,1)S(1)} collective-permute-done((bf16[768,512]{1,0:T(8,128)(2,1)S(1)}, bf16[768,512]{1,0:T(8,128)(2,1)S(1)}, u32[]{:S(2)}, u32[]{:S(2)}) %collective-permute-start.6) | collective-permute-done | bytes 786464 | tf_op jit(solution)/shard_map/ppermute | solution.py:23
  147.0 2.2 broadcast_select_fusion.1
  149.2 3.6 %convolution_convert_fusion = bf16[1024,1536]{1,0:T(8,128)(2,1)S(1)} fusion(bf16[1024,1024]{1,0:T(8,128)(2,1)S(1)} %bitcast.88, bf16[512,1536]{1,0:T(8,128)(2,1)S(1)} %get-tuple-element.15, bf16[512,1536]{1,0:T(8,128)(2,1)S(1)} %get-tuple-element.14), kind=kOutput, calls=%fused_computation.1 | convolution fusion | flops 3229089792 | bytes 8388608 | tf_op jit(solution)/shard_map/dot_general | solution.py:606
  152.8 52.9 %shard_map.172 = bf16[3,8,32,1536]{3,2,1,0:T(8,128)(2,1)S(1)} custom-call(bf16[4,8,32,1536]{3,2,1,0:T(8,128)(2,1)S(1)} %bitcast.80), custom_call_target="tpu_custom_call" | custom-call | tf_op jit(solution)/shard_map/pallas_call | solution.py:199
  206.1 1.0 fusion.11
  207.1 27.8 %shard_map.173 = bf16[4,2,128,768]{3,2,1,0:T(8,128)(2,1)} custom-call(bf16[2,128,768]{2,1,0:T(8,128)(2,1)} %bitcast.93), custom_call_target="tpu_custom_call" | custom-call | tf_op jit(solution)/shard_map/pallas_call | solution.py:266
  234.9 3.2 %convolution_convert_fusion.2 = bf16[1024,1024]{1,0:T(8,128)(2,1)S(1)} fusion(bf16[1024,768]{1,0:T(8,128)(2,1)} %bitcast.92, bf16[768,512]{1,0:T(8,128)(2,1)S(1)} %get-tuple-element.17, bf16[768,512]{1,0:T(8,128)(2,1)S(1)} %get-tuple-element.16), kind=kOutput, calls=%fused_computation.6 | convolution fusion | flops 1614807040 | bytes 5242880 | tf_op jit(solution)/shard_map/dot_general | solution.py:612
  238.1 16.2 %shard_map.174 = bf16[5,4,32,1024]{3,2,1,0:T(8,128)(2,1)S(1)} custom-call(bf16[4,8,32,1024]{3,2,1,0:T(8,128)(2,1)S(1)} %bitcast.81), custom_call_target="tpu_custom_call" | custom-call | tf_op jit(solution)/shard_map/pallas_call | solution.py:199
  254.4 1.0 reduce_sum.75.rows_ref
  255.4 8.9 %shard_map.175 = bf16[4,32,1024]{2,1,0:T(8,128)(2,1)} custom-call(bf16[4,32,1024]{2,1,0:T(8,128)(2,1)} %reduce_sum.75.rows_ref), custom_call_target="tpu_custom_call" | custom-call | tf_op jit(solution)/shard_map/pallas_call | solution.py:110
  264.3 1.0 convert_bitcast_fusion
  (133 shorter events, 18.0 us)
Async XLA Ops:
  0.6 5.5 %copy-start.26 = (bf16[128]{0:T(256)(128)(2,1)S(1)}, bf16[128]{0:T(256)(128)(2,1)}, u32[]{:S(2)}) copy-start(bf16[128]{0:T(256)(128)(2,1)} %param.25) | copy-start | bytes 772
  2.7 3.4 %copy-start.24 = (f32[64]{0:T(128)}, f32[64]{0:T(128)S(1)}, u32[]{:S(2)}) copy-start(f32[64]{0:T(128)S(1)} %get-tuple-element.33) | copy-start | bytes 772
  2.7 12.8 %copy-start.17 = (f32[64,64]{1,0:T(8,128)}, f32[64,64]{1,0:T(8,128)S(1)}, u32[]{:S(2)}) copy-start(f32[64,64]{1,0:T(8,128)S(1)} %get-tuple-element.34) | copy-start | bytes 49156
  2.8 12.7 %copy-start.22 = (s32[64]{0:T(128)}, s32[64]{0:T(128)S(1)}, u32[]{:S(2)}) copy-start(s32[64]{0:T(128)S(1)} %pad_add_fusion) | copy-start | bytes 772
  6.7 5.8 %copy-start.13 = (bf16[512,1536]{1,0:T(8,128)(2,1)S(1)}, bf16[512,1536]{1,0:T(8,128)(2,1)}, u32[]{:S(2)}) copy-start(bf16[512,1536]{1,0:T(8,128)(2,1)} %param.30) | copy-start | bytes 4718596
  6.7 5.8 %copy-start.14 = (bf16[512,1536]{1,0:T(8,128)(2,1)S(1)}, bf16[512,1536]{1,0:T(8,128)(2,1)}, u32[]{:S(2)}) copy-start(bf16[512,1536]{1,0:T(8,128)(2,1)} %param.29) | copy-start | bytes 4718596
  7.2 12.4 %collective-permute-start = (bf16[32,4096]{1,0:T(8,128)(2,1)S(1)}, bf16[32,4096]{1,0:T(8,128)(2,1)}, u32[]{:S(2)}, u32[]{:S(2)}) collective-permute-start(bf16[32,4096]{1,0:T(8,128)(2,1)S(1)} %bitcast.97), channel_id=1, source_target_pairs={{0,1},{1,0},{2,3},{3,2},{4,5},{5,4},{6,7},{7,6},{8,9},{9,8},{10,11... | collective-permute-start | bytes 786440 | tf_op jit(solution)/shard_map/ppermute | solution.py:23
  9.6 63.0 %collective-permute-start.4 = (bf16[512,512]{1,0:T(8,128)(2,1)}, bf16[512,512]{1,0:T(8,128)(2,1)}, u32[]{:S(2)}, u32[]{:S(2)}) collective-permute-start(bf16[512,512]{1,0:T(8,128)(2,1)} %constant_dynamic-slice_fusion.5), channel_id=1, source_target_pairs={{0,4},{4,0},{8,12},{12,8},{16,20},{20,16},{24,28},{28,24},{1,5},{5... | collective-permute-start | bytes 1572872 | tf_op jit(solution)/shard_map/ppermute | solution.py:23
  13.8 2.0 copy-start.11
  15.1 2.4 copy-start.6
  15.1 3.7 %copy-start.28 = (s32[16]{0:T(128)S(1)}, s32[16]{0:T(128)}, u32[]{:S(2)}) copy-start(s32[16]{0:T(128)} %param.24) | copy-start | bytes 196
  15.1 131.9 %collective-permute-start.5 = (bf16[512,1536]{1,0:T(8,128)(2,1)}, bf16[512,1536]{1,0:T(8,128)(2,1)}, u32[]{:S(2)}, u32[]{:S(2)}) collective-permute-start(bf16[512,1536]{1,0:T(8,128)(2,1)} %pad_maximum_fusion.1), channel_id=1, source_target_pairs={{0,4},{4,0},{8,12},{12,8},{16,20},{20,16},{24,28},{28,24},{1,5},{5... | collective-permute-start | bytes 4718600 | tf_op jit(solution)/shard_map/ppermute | solution.py:23
  15.2 5.5 %copy-start.1 = (bf16[1024,1024]{1,0:T(8,128)(2,1)S(1)}, bf16[1024,1024]{1,0:T(8,128)(2,1)}, u32[]{:S(2)}) copy-start(bf16[1024,1024]{1,0:T(8,128)(2,1)} %key_ref.1) | copy-start | bytes 6291460
  20.7 1.6 copy-start.2
  35.1 4.7 %copy-start.18 = (f32[64,64]{1,0:T(8,128)S(1)}, f32[64,64]{1,0:T(8,128)}, u32[]{:S(2)}) copy-start(f32[64,64]{1,0:T(8,128)} %copy-done.17) | copy-start | bytes 49156
  35.1 5.4 %copy-start.21 = (bf16[4096]{0:T(1024)(128)(2,1)S(1)}, bf16[4096]{0:T(1024)(128)(2,1)}, u32[]{:S(2)}) copy-start(bf16[4096]{0:T(1024)(128)(2,1)} %param.27) | copy-start | bytes 24580
  36.2 4.4 %copy-start.5 = (f32[8,256,128]{2,1,0:T(8,128)S(1)}, f32[8,256,128]{2,1,0:T(8,128)}, u32[]{:S(2)}) copy-start(f32[8,256,128]{2,1,0:T(8,128)} %copy-done.4) | copy-start | bytes 3145732
  37.0 4.6 %collective-permute-start.2 = (bf16[8,4,32,128]{3,1,0,2:T(4,128)(2,1)}, bf16[8,4,32,128]{3,1,0,2:T(4,128)(2,1)}, u32[]{:S(2)}, u32[]{:S(2)}) collective-permute-start(bf16[8,4,32,128]{3,1,0,2:T(4,128)(2,1)} %copy.67), channel_id=1, source_target_pairs={{0,1},{1,0},{2,3},{3,2},{4,5},{5,4},{6,7},{7,6},{8,9},{9,8},{10,11... | collective-permute-start | bytes 786440 | tf_op jit(solution)/shard_map/ppermute | solution.py:23
  38.8 1.9 collective-permute-start.1
  39.8 1.4 collective-permute-start.3
  40.6 87.5 %collective-permute-start.7 = (bf16[32,2048]{1,0:T(8,128)(2,1)}, bf16[32,2048]{1,0:T(8,128)(2,1)}, u32[]{:S(2)}, u32[]{:S(2)}) collective-permute-start(bf16[32,2048]{1,0:T(8,128)(2,1)} %constant_dynamic-update-slice_fusion), channel_id=1, source_target_pairs={{0,1},{1,0},{2,3},{3,2},{4,5},{5,4},{6,7},{7,6},{8,9},{9,8},{10,11... | collective-permute-start | bytes 393224 | tf_op jit(solution)/shard_map/ppermute | solution.py:23
  41.6 31.0 %copy-start.15 = (bf16[512,1024]{1,0:T(8,128)(2,1)S(1)}, bf16[512,1024]{1,0:T(8,128)(2,1)}, u32[]{:S(2)}) copy-start(bf16[512,1024]{1,0:T(8,128)(2,1)} %param.28) | copy-start | bytes 3145732
  72.6 1.7 copy-start.10
  97.6 9.1 %copy-start.19 = (bf16[32,4096]{1,0:T(8,128)(2,1)S(1)}, bf16[32,4096]{1,0:T(8,128)(2,1)}, u32[]{:S(2)}) copy-start(bf16[32,4096]{1,0:T(8,128)(2,1)} %param.16) | copy-start | bytes 786436
  106.8 19.9 %copy-start.16 = (bf16[768,512]{1,0:T(8,128)(2,1)S(1)}, bf16[768,512]{1,0:T(8,128)(2,1)}, u32[]{:S(2)}) copy-start(bf16[768,512]{1,0:T(8,128)(2,1)} %constant_dynamic-slice_fusion.4) | copy-start | bytes 2359300
  106.8 21.1 %copy-start.25 = (f32[64]{0:T(128)S(1)}, f32[64]{0:T(128)}, u32[]{:S(2)}) copy-start(f32[64]{0:T(128)} %copy-done.24) | copy-start | bytes 772
  106.8 21.1 %copy-start.23 = (s32[64]{0:T(128)S(1)}, s32[64]{0:T(128)}, u32[]{:S(2)}) copy-start(s32[64]{0:T(128)} %copy-done.22) | copy-start | bytes 772
  106.8 39.8 %copy-start.12 = (bf16[1536,512]{1,0:T(8,128)(2,1)S(1)}, bf16[1536,512]{1,0:T(8,128)(2,1)}, u32[]{:S(2)}) copy-start(bf16[1536,512]{1,0:T(8,128)(2,1)} %param.31) | copy-start | bytes 4718596
  126.7 20.3 %copy-start.7 = (bf16[512,768]{1,0:T(8,128)(2,1)S(1)}, bf16[512,768]{1,0:T(8,128)(2,1)}, u32[]{:S(2)}) copy-start(bf16[512,768]{1,0:T(8,128)(2,1)} %get-tuple-element.20) | copy-start | bytes 2359300
  126.7 20.3 %copy-start.8 = (bf16[512,768]{1,0:T(8,128)(2,1)S(1)}, bf16[512,768]{1,0:T(8,128)(2,1)}, u32[]{:S(2)}) copy-start(bf16[512,768]{1,0:T(8,128)(2,1)} %get-tuple-element.38) | copy-start | bytes 2359300
  126.7 19.9 %collective-permute-start.6 = (bf16[768,512]{1,0:T(8,128)(2,1)S(1)}, bf16[768,512]{1,0:T(8,128)(2,1)S(1)}, u32[]{:S(2)}, u32[]{:S(2)}) collective-permute-start(bf16[768,512]{1,0:T(8,128)(2,1)S(1)} %copy-done.16), channel_id=1, source_target_pairs={{0,4},{4,0},{8,12},{12,8},{16,20},{20,16},{24,28},{28,24},{1,5},{5... | collective-permute-start | bytes 2359304 | tf_op jit(solution)/shard_map/ppermute | solution.py:23
  147.0 2.2 copy-start.9
  (5 other events, 5.4 us)
